TPU v7x, 512 devices: a whole 4x4x16 slice. The times are simulated.
512 devices in a mesh: dp: 32 (over z_lo, x), mp: 16 (over z_hi, y, core).
Axes of the slice: x: 4, y: 4, z: 16 (z_hi: 2, z_lo: 8; z = z_hi * 8 + z_lo), core: 2. Of those that a mesh axis runs over, the one named last changes fastest.
Arguments:
- x_tiles: bfloat16 [32768, 6144], P('dp', 'mp')
- counts: int32 [32, 32], replicated, may hold values from 4 to 28, as said below
- owners: int32 [32, 32], replicated, may hold values from 0 to 31, as said below
- ln_gain: bfloat16 [6144], P('mp'), may hold values from 0.5 to 1.5
- w_up: bfloat16 [6144, 12288], P('dp', 'mp'), may hold values from -0.078125 to 0.078125
- up_bias: bfloat16 [12288], P('mp'), may hold values from -3 to 3
Outputs:
- hidden_act: bfloat16 [16384, 12288], P('dp', 'mp')
Inputs may be any that keep to these rules, and one draw needn't show every extreme that they name: Each row of owners is a permutation of 0 .. 31. Tile t of group s holds counts[s, t] patches in its first slots; every group takes exactly 512 patches in all.
All inputs are finite; a program needn't handle non-finite values.
Results may differ from a plain program's by a relative error of at most 0.0047.
Values may be sent and summed in bfloat16 or wider, within the bound.
No kernel may reach another device: no remote copies, remote signals or barrier semaphores. Data moves between devices by JAX's collectives and lax.ppermute only.
A program may use at most 64 MiB of HBM per device.

v0:
```python
import jax
import jax.numpy as jnp
from jax import lax
from jax.sharding import PartitionSpec as P

D = 6144
RECV = 512


def local(x_tiles, counts, owners, ln_gain, w_up, up_bias):
    groups = lax.axis_size("dp")
    my_index = lax.axis_index("dp")
    tile_rows = x_tiles.shape[0] // groups
    width_part = x_tiles.shape[1]
    tile_block = x_tiles.reshape(groups, tile_rows, width_part)
    inverse = jnp.argsort(owners, axis=1)
    my_tiles = lax.dynamic_index_in_dim(inverse, my_index, 0, keepdims=False)
    outgoing = jnp.take(tile_block, my_tiles, axis=0)
    incoming = lax.all_to_all(outgoing, "dp", split_axis=0, concat_axis=0, tiled=True)
    slot_count = incoming.shape[1]
    source_tiles = lax.dynamic_index_in_dim(inverse, my_index, 1, keepdims=False)
    held_rows = jnp.take_along_axis(counts, source_tiles[:, None], axis=1)[:, 0]
    inclusive = jnp.cumsum(held_rows)
    exclusive = inclusive - held_rows
    positions = jnp.arange(RECV, dtype=jnp.int32)
    source = jnp.sum((inclusive[None, :] <= positions[:, None]).astype(jnp.int32), axis=1)
    slot_index = positions - jnp.take(exclusive, source)
    flat_index = source * slot_count + slot_index
    packed = jnp.take(incoming.reshape(groups * slot_count, width_part), flat_index, axis=0)
    as_float = packed.astype(jnp.float32)
    row_sum, row_square = lax.psum(
        (jnp.sum(as_float, axis=1), jnp.sum(as_float * as_float, axis=1)), "mp"
    )
    row_mean = row_sum / D
    variance = row_square / D - row_mean * row_mean
    scaled = (
        (as_float - row_mean[:, None])
        * lax.rsqrt(variance + 1e-06)[:, None]
        * ln_gain.astype(jnp.float32)
    )
    normed = lax.all_gather(scaled.astype(jnp.bfloat16), "mp", axis=1, tiled=True)
    projected = jnp.dot(
        normed, lax.all_gather(w_up, "dp", axis=0, tiled=True), preferred_element_type=jnp.float32
    )
    return jax.nn.gelu(projected + up_bias.astype(jnp.float32), approximate=False).astype(
        jnp.bfloat16
    )


def solution(mesh):
    return jax.shard_map(
        local,
        mesh=mesh,
        in_specs=(P("dp", "mp"), P(), P(), P("mp"), P("dp", "mp"), P("mp")),
        out_specs=P("dp", "mp"),
        check_vma=False,
    )
```

profile of v0, /device:TPU:2, one launch (start us, length us, event | category | flops | bytes accessed | tf_op | source)
XLA Modules:
  0.0 536.9 jit_solution(3228038346032233318)
XLA Ops:
  6.5 0.0 copy-start
  6.5 0.9 copy.10
  7.4 0.8 sort.17
  8.2 0.2 dynamic-slice_reduce_fusion
  8.5 0.0 copy-done
  8.5 0.7 gather_fusion
  9.2 0.0 copy-start.3
  9.2 0.0 copy-start.1
  9.2 1.0 broadcast_select_fusion
  10.3 15.7 %all-to-all-start = ((bf16[32,32,384]{2,1,0:T(8,128)(2,1)}), bf16[32,32,384]{2,1,0:T(8,128)(2,1)S(1)}, u32[]{:S(2)}, u32[]{:S(2)}) async-start(bf16[32,32,384]{2,1,0:T(8,128)(2,1)} %broadcast_select_fusion), calls=%async_computation | async-start | bytes 1572864 | tf_op jit(solution)/shard_map/all_to_all | solution.py:19
  26.0 0.0 all-gather.3.cloned.1.call-start
  26.0 0.0 copy-done.3
  26.0 0.0 copy-done.1
  26.0 0.7 gather_fusion.2
  26.8 0.1 copy.11
  26.9 0.1 reduce-window.8
  26.9 0.1 reduce
  27.0 0.7 fusion.18
  27.8 0.7 fusion.17
  28.5 0.1 convert_reduce_fusion.1
  28.6 4.4 compare_select_fusion.2
  33.0 0.2 compare_reduce_fusion.24
  33.1 15.7 %compare_and_fusion.1 = (pred[512]{0:T(512)(128)(4,1)S(1)}, s32[512]{0:T(512)S(1)}) fusion(s32[512]{0:T(512)S(1)} %convert_reduce_fusion.1, pred[512]{0:T(512)(128)(4,1)S(1)} %get-tuple-element.33, pred[512]{0:T(512)(128)(4,1)S(1)} %get-tuple-element.31, pred[512]{0:T(512)(128)(4,1)S(1)} %get-tuple-element.32, pred[512]{0:T(512)(128)(4,1)S(1)} %get-tuple-element.30, ...), kind=kLoop, calls=%fused_computation.79 | loop fusion | flops 20992 | bytes 19556 | tf_op jit(solution)/shard_map/jit(_take)/and | solution.py:29
  48.8 16.4 %all-to-all-done = bf16[32,32,384]{2,1,0:T(8,128)(2,1)S(1)} async-done(((bf16[32,32,384]{2,1,0:T(8,128)(2,1)}), bf16[32,32,384]{2,1,0:T(8,128)(2,1)S(1)}, u32[]{:S(2)}, u32[]{:S(2)}) %all-to-all-start) | async-done | bytes 786464 | tf_op jit(solution)/shard_map/all_to_all | solution.py:19
  65.3 1.9 gather_fusion.1
  67.2 0.0 copy-start.2
  67.2 0.4 convert_reduce_fusion
  67.6 67.1 %all-reduce = (f32[512]{0:T(512)S(1)}, f32[512]{0:T(512)S(1)}) all-reduce(f32[512]{0:T(512)S(1)} %get-tuple-element.8, f32[512]{0:T(512)S(1)} %get-tuple-element.7), channel_id=1, replica_groups=mesh['dp'=32,'mp'=16] {'mp'}, use_global_device_ids=true, to_apply=%region_6.7 | all-reduce | flops 1024 | bytes 8192 | tf_op jit(solution)/shard_map/psum | solution.py:31
  134.7 1.0 fusion.12
  135.8 0.0 all-gather.3.cloned.1.call-update
  135.8 0.0 all-gather.5.cloned.1.call-start
  135.8 0.7 all-gather.5.cloned.1.call-update
  136.5 0.0 copy-done.2
  136.5 140.3 %all-gather.3.cloned.1.call-done = bf16[512,6144]{1,0:T(8,128)(2,1)} async-done(((bf16[512,384]{1,0:T(8,128)(2,1)}), bf16[512,6144]{1,0:T(8,128)(2,1)}) %all-gather.3.cloned.1.call-update) | async-done | bytes 6291472 | tf_op jit(solution)/shard_map/all_gather | solution.py:41
  276.8 239.5 %all-gather.5.cloned.1.call-done = bf16[6144,768]{1,0:T(8,128)(2,1)} async-done(((bf16[192,768]{1,0:T(8,128)(2,1)}), bf16[6144,768]{1,0:T(8,128)(2,1)}) %all-gather.5.cloned.1.call-update) | async-done | bytes 9437200 | tf_op jit(solution)/shard_map/all_gather | solution.py:43
  516.4 13.7 %fusion.2 = bf16[512,768]{1,0:T(8,128)(2,1)} fusion(bf16[512,6144]{1,0:T(8,128)(2,1)} %all-gather.3.cloned.1.call-done, bf16[6144,768]{1,0:T(8,128)(2,1)} %all-gather.5.cloned.1.call-done, f32[768]{0:T(1024)S(1)} %convert_element_type.22), kind=kOutput, calls=%fused_computation.6 | convolution fusion | flops 4857790464 | bytes 16518144 | tf_op jit(solution)/shard_map/dot_general | solution.py:42
  (14 shorter events, 0.1 us)
Async XLA Ops:
  6.5 1.9 copy-start
  9.2 16.8 %copy-start.3 = (bf16[384]{0:T(512)(128)(2,1)S(1)}, bf16[384]{0:T(512)(128)(2,1)}, u32[]{:S(2)}) copy-start(bf16[384]{0:T(512)(128)(2,1)} %param.9) | copy-start | bytes 2308
  9.2 16.8 %copy-start.1 = (s32[32,32]{1,0:T(8,128)S(1)}, s32[32,32]{1,0:T(8,128)}, u32[]{:S(2)}) copy-start(s32[32,32]{1,0:T(8,128)} %param.7) | copy-start | bytes 12292
  10.3 55.0 %all-to-all-start = ((bf16[32,32,384]{2,1,0:T(8,128)(2,1)}), bf16[32,32,384]{2,1,0:T(8,128)(2,1)S(1)}, u32[]{:S(2)}, u32[]{:S(2)}) async-start(bf16[32,32,384]{2,1,0:T(8,128)(2,1)} %broadcast_select_fusion), calls=%async_computation | async-start | bytes 1572864 | tf_op jit(solution)/shard_map/all_to_all | solution.py:19
  26.0 250.9 %all-gather.3.cloned.1.call-start = ((), (), s32[]{:S(2)}) async-start(), calls=%async_computation.1 | async-start | bytes 6684672 | tf_op jit(solution)/shard_map/all_gather | solution.py:41
  67.2 69.3 %copy-start.2 = (bf16[768]{0:T(1024)(128)(2,1)S(1)}, bf16[768]{0:T(1024)(128)(2,1)}, u32[]{:S(2)}) copy-start(bf16[768]{0:T(1024)(128)(2,1)} %param.11) | copy-start | bytes 4612
  135.8 380.6 %all-gather.5.cloned.1.call-start = ((), (), s32[]{:S(2)}) async-start(), calls=%async_computation.2 | async-start | bytes 9732096 | tf_op jit(solution)/shard_map/all_gather | solution.py:43
Sparse Core Ops, SparseCore 0:
  135.9 140.8 all-gather.2
  278.9 237.4 all-gather.4
where the time goes:
time: 537 us
  waiting for transfers between devices  397 us (74%)
  blocking collectives  67.1 us (12%)
  other arithmetic  23.8 us (4%)
  starting transfers between devices  15.8 us (3%)
  matrix products  13.7 us (3%)
  between operations  13.6 us (3%)
  local copies, waits for them, and re-layouts  5.97 us (1%)
    all_gather x1, waiting for transfers between devices, local(): lax.all_gather(w_up, 'dp', axis=0, tiled=True)  240 us
    all_gather x1, waiting for transfers between devices, local(): lax.all_gather(scaled.astype(jnp.bfloat16), 'mp', axis=1, tiled=True)  140 us
    psum x1, blocking collectives, local(): lax.psum((jnp.sum(as_float, axis=1), jnp.sum(as_float * as_float, axis=1)...  67.1 us
    all_to_all x1, waiting for transfers between devices, local(): lax.all_to_all(outgoing, 'dp', split_axis=0, concat_axis=0, tiled=True)  16.4 us
    and x1, other arithmetic, local(): jnp.take(incoming.reshape(groups * slot_count, width_part), flat_index, a...  15.7 us
    all_to_all x1, starting transfers between devices, local(): lax.all_to_all(outgoing, 'dp', split_axis=0, concat_axis=0, tiled=True)  15.7 us
    dot_general x1, matrix products, local(): jnp.dot(normed, lax.all_gather(w_up, 'dp', axis=0, tiled=True), preferred...  13.7 us
  transfers between devices with their start and end apart: 3, of which 3 were waited for; matrix products, arithmetic and copies ran while one was open for 4% of the time, Pallas kernels for 0%

commit v1 on v0

v1 whole, which is shorter than its diff:
```python
import functools

import jax
import jax.numpy as jnp
from jax import lax
from jax.experimental import pallas as pl
from jax.experimental.pallas import tpu as pltpu
from jax.sharding import Mesh, PartitionSpec as P

D = 6144
RECV = 512
PART = 384
BLOCK = 192
HALF = BLOCK // 2
COLS = 768
GAIN_ROWS = 16
ROWS = RECV + GAIN_ROWS
STRIP = 32
INV_SQRT2 = 0.7071067811865476


def shift(value, axis, size, step):
    return lax.ppermute(value, axis, [(i, (i + step) % size) for i in range(size)])


def row_copies(x, pieces, w_all, sems):
    copies = []
    for half in range(2):
        own, below, above, far_a, far_b = pieces[5 * half : 5 * half + 5]
        sources = [(own, z, 0, z) for z in range(8)]
        sources += [(below, z, 3, z) for z in range(8)]
        sources += [(above, z, 1, z) for z in range(8)]
        sources += [(far_a, z, 2, z) for z in range(4)]
        sources += [(far_b, z - 4, 2, z) for z in range(4, 8)]
        for ref, at, step, z in sources:
            block = 4 * z + lax.rem(x + step, 4)
            start = pl.multiple_of(block * BLOCK + half * HALF, 32)
            copies.append(
                pltpu.make_async_copy(
                    ref.at[pl.ds(at * HALF, HALF), :],
                    w_all.at[pl.ds(start, HALF), :],
                    sems.at[len(copies)],
                )
            )
    return copies


def mlp_kernel(place_ref, near_ref, far_ref, bias_ref, *refs):
    pieces, (out_ref, w_all, normed, sems) = refs[:10], refs[10:]
    x, half = place_ref[0], place_ref[1]
    copies = row_copies(x, pieces, w_all, sems)
    for copy in copies:
        copy.start()

    chunks = [
        (ref, c, y, side)
        for side, ref in enumerate((near_ref, far_ref))
        for y in range(4)
        for c in range(2)
    ]

    @pl.loop(0, RECV // STRIP)
    def _(strip):
        rows = pl.ds(pl.multiple_of(strip * STRIP, STRIP), STRIP)
        total = jnp.zeros((STRIP, 128), jnp.float32)
        square = jnp.zeros((STRIP, 128), jnp.float32)
        for ref, c, y, _side in chunks:
            for lane in range(PART // 128):
                v = ref[c, y, rows, lane * 128 : (lane + 1) * 128].astype(jnp.float32)
                total += v
                square += v * v
        row_mean = jnp.sum(total, axis=1, keepdims=True) / D
        variance = jnp.sum(square, axis=1, keepdims=True) / D - row_mean * row_mean
        scale = lax.rsqrt(variance + 1e-06)
        for ref, c, y, side in chunks:
            v = ref[c, y, rows, :].astype(jnp.float32)
            gain = ref[c, y, RECV : RECV + 1, :].astype(jnp.float32)
            at = 8 * lax.rem(half + side, 2) + 2 * y + c
            columns = pl.ds(pl.multiple_of(at * PART, 128), PART)
            normed[rows, columns] = ((v - row_mean) * scale * gain).astype(jnp.bfloat16)

    for copy in copies:
        copy.wait()
    for n in range(COLS // 256):
        cols = slice(n * 256, (n + 1) * 256)
        v = jnp.dot(normed[...], w_all[:, cols], preferred_element_type=jnp.float32)
        v = v + bias_ref[:, cols].astype(jnp.float32)
        out_ref[:, cols] = (v * (1.0 + lax.erf(v * INV_SQRT2)) * 0.5).astype(jnp.bfloat16)


def mlp(place, near, far, bias, pieces):
    vmem = pl.BlockSpec(memory_space=pltpu.VMEM)
    return pl.pallas_call(
        mlp_kernel,
        out_shape=jax.ShapeDtypeStruct((RECV, COLS), jnp.bfloat16),
        in_specs=[pl.BlockSpec(memory_space=pltpu.SMEM), vmem, vmem, vmem]
        + [pl.BlockSpec(memory_space=pl.ANY)] * len(pieces),
        out_specs=vmem,
        scratch_shapes=[
            pltpu.VMEM((D, COLS), jnp.bfloat16),
            pltpu.VMEM((RECV, D), jnp.bfloat16),
            pltpu.SemaphoreType.DMA((64,)),
        ],
        compiler_params=pltpu.CompilerParams(vmem_limit_bytes=44 * 1024 * 1024),
        cost_estimate=pl.CostEstimate(
            flops=2 * RECV * D * COLS, bytes_accessed=2 * (RECV * D + D * COLS), transcendentals=RECV * COLS
        ),
    )(place, near, far, bias, *pieces)


def gather_weight(w_half):
    own = lax.all_gather(w_half, "zl", axis=0, tiled=True)
    below = shift(own, "x", 4, 1)
    above = shift(own, "x", 4, -1)
    middle = own.shape[0] // 2
    return [own, below, above, shift(below[:middle], "x", 4, 1), shift(above[middle:], "x", 4, -1)]


def spread(rows):
    copies = jnp.broadcast_to(rows[None], (4,) + rows.shape)
    along_y = lax.all_to_all(copies, "y", split_axis=0, concat_axis=0, tiled=True)
    return lax.all_gather(along_y, "c", axis=0)


def local(x_tiles, counts, owners, ln_gain, w_up, up_bias):
    pieces = gather_weight(w_up[:HALF]) + gather_weight(w_up[HALF:])

    groups = 32
    my_index = lax.axis_index("zl") * 4 + lax.axis_index("x")
    slots = x_tiles.shape[0] // groups
    tile_block = x_tiles.reshape(groups, slots, PART)
    inverse = jnp.argsort(owners, axis=1)
    my_tiles = lax.dynamic_index_in_dim(inverse, my_index, 0, keepdims=False)
    outgoing = jnp.take(tile_block, my_tiles, axis=0)
    incoming = lax.all_to_all(outgoing, ("zl", "x"), split_axis=0, concat_axis=0, tiled=True)
    source_tiles = lax.dynamic_index_in_dim(inverse, my_index, 1, keepdims=False)
    held_rows = jnp.take_along_axis(counts, source_tiles[:, None], axis=1)[:, 0]
    inclusive = jnp.cumsum(held_rows)
    exclusive = inclusive - held_rows
    positions = jnp.arange(RECV, dtype=jnp.int32)
    source = jnp.sum((inclusive[None, :] <= positions[:, None]).astype(jnp.int32), axis=1)
    slot_index = positions - jnp.take(exclusive, source)
    flat_index = source * slots + slot_index
    packed = jnp.take(incoming.reshape(groups * slots, PART), flat_index, axis=0)

    gains = jnp.broadcast_to(ln_gain[None, :], (GAIN_ROWS, PART))
    mine = jnp.concatenate([packed, gains], axis=0)
    other = shift(mine, "zh", 2, 1)
    near, far = spread(mine), spread(other)
    place = jnp.stack([lax.axis_index("x"), lax.axis_index("zh")]).astype(jnp.int32)
    return mlp(place, near, far, up_bias[None, :], pieces)


def solution(mesh):
    fine = Mesh(mesh.devices.reshape(8, 4, 2, 4, 2), ("zl", "x", "zh", "y", "c"))
    dp, mp = ("zl", "x"), ("zh", "y", "c")
    return jax.shard_map(
        local,
        mesh=fine,
        in_specs=(P(dp, mp), P(), P(), P(mp), P(dp, mp), P(mp)),
        out_specs=P(dp, mp),
        check_vma=False,
    )
```

time: 537 us -> 310 us (0.58)
  the two profiles are of different devices: /device:TPU:2 before, /device:TPU:32 now
where the time goes in v1:
time: 310 us; the launch traced here: 309 us
  waiting for transfers between devices  127 us (41%)
  starting transfers between devices  57.5 us (19%)
  blocking collectives  44.8 us (14%)
  Pallas kernels  25.6 us (8%)
  other arithmetic  22.3 us (7%)
  local copies, waits for them, and re-layouts  18.6 us (6%)
  between operations  13.5 us (4%)
    ppermute x9, waiting for transfers between devices, shift(): lax.ppermute(value, axis, [(i, (i + step) % size) for i in range(size)])  91.7 us
    all_to_all x2, blocking collectives, spread(): lax.all_to_all(copies, 'y', split_axis=0, concat_axis=0, tiled=True)  44.8 us
    ppermute x9, starting transfers between devices, shift(): lax.ppermute(value, axis, [(i, (i + step) % size) for i in range(size)])  42.2 us
    all_to_all x1, waiting for transfers between devices, local(): lax.all_to_all(outgoing, ('zl', 'x'), split_axis=0, concat_axis=0, tiled=...  34.6 us
    pallas_call x1, Pallas kernels, mlp(): pl.pallas_call(mlp_kernel, out_shape=jax.ShapeDtypeStruct((RECV, COLS), j...  25.6 us
    and x1, other arithmetic, local(): jnp.take(incoming.reshape(groups * slots, PART), flat_index, axis=0)  15.5 us
    all_to_all x1, starting transfers between devices, local(): lax.all_to_all(outgoing, ('zl', 'x'), split_axis=0, concat_axis=0, tiled=...  15.2 us
    unnamed x22, local copies, waits for them, and re-layouts  7.97 us
  transfers between devices with their start and end apart: 14, of which 8 were waited for; matrix products, arithmetic and copies ran while one was open for 10% of the time, Pallas kernels for 0%

profile of v1, /device:TPU:32, one launch (start us, length us, event | category | flops | bytes accessed | tf_op | source)
XLA Modules:
  0.0 309.5 jit_solution(15846337799055377750)
XLA Ops:
  6.5 1.8 fusion.3
  8.4 0.8 copy.12
  9.2 0.8 sort.17
  10.0 0.2 dynamic-slice_reduce_fusion
  10.2 0.7 gather_fusion
  11.0 1.0 broadcast_select_fusion
  12.0 15.2 %all-to-all-start = ((bf16[32,32,384]{2,1,0:T(8,128)(2,1)}), bf16[32,32,384]{2,1,0:T(8,128)(2,1)S(1)}, u32[]{:S(2)}, u32[]{:S(2)}) async-start(bf16[32,32,384]{2,1,0:T(8,128)(2,1)} %broadcast_select_fusion), calls=%async_computation | async-start | bytes 1572864 | tf_op jit(solution)/shard_map/all_to_all | solution.py:135
  27.3 0.7 all-gather.9.cloned.1.call-update
  28.1 0.7 gather_fusion.2
  29.1 0.7 fusion.5
  29.8 0.7 fusion.4
  30.6 4.2 %compare_select_fusion.2 = (s32[512,1]{0,1:T(1,128)S(1)}, s32[512,1]{0,1:T(1,128)S(1)}) fusion(s32[]{:T(128)} %bitcast.33, s32[]{:T(128)} %bitcast.34, s32[]{:T(128)} %bitcast.35, s32[]{:T(128)} %bitcast.36, s32[]{:T(128)} %bitcast.37, s32[]{:T(128)} %bitcast.39, s32[]{:T(128)} %bitcast.38, s32[512,1]{0,1:T(1,128)S(1)} %bitcast.58), kind=kLoop, calls=%fused_computation.36 | loop fusion | flops 7680 | bytes 6172 | tf_op jit(solution)/shard_map/jit(_take)/gather | solution.py:142
  34.8 0.2 compare_reduce_fusion.24
  35.0 15.5 %compare_and_fusion.1 = (pred[512]{0:T(512)(128)(4,1)S(1)}, s32[512]{0:T(512)S(1)}) fusion(s32[512]{0:T(512)S(1)} %convert_reduce_fusion, pred[512]{0:T(512)(128)(4,1)S(1)} %get-tuple-element.31, pred[512]{0:T(512)(128)(4,1)S(1)} %get-tuple-element.29, pred[512]{0:T(512)(128)(4,1)S(1)} %get-tuple-element.30, pred[512]{0:T(512)(128)(4,1)S(1)} %get-tuple-element.28, ...), kind=kLoop, calls=%fused_computation.53 | loop fusion | flops 20992 | bytes 19556 | tf_op jit(solution)/shard_map/jit(_take)/and | solution.py:144
  50.5 34.6 %all-to-all-done = bf16[32,32,384]{2,1,0:T(8,128)(2,1)S(1)} async-done(((bf16[32,32,384]{2,1,0:T(8,128)(2,1)}), bf16[32,32,384]{2,1,0:T(8,128)(2,1)S(1)}, u32[]{:S(2)}, u32[]{:S(2)}) %all-to-all-start) | async-done | bytes 786464 | tf_op jit(solution)/shard_map/all_to_all | solution.py:135
  85.1 1.9 gather_fusion.1
  87.1 0.1 broadcast_select_fusion.1
  87.3 0.1 broadcast_in_dim.64
  87.4 21.9 %all_to_all.15 = bf16[4,528,384]{2,1,0:T(8,128)(2,1)} all-to-all(bf16[4,528,384]{2,1,0:T(8,128)(2,1)S(1)} %broadcast_in_dim.64), channel_id=1, replica_groups=mesh['zl'=8,'x'=4,'zh'=2,'y'=4,'c'=2] {'y'}, dimensions={0} | all-to-all | bytes 3244032 | tf_op jit(solution)/shard_map/all_to_all | solution.py:121
  109.4 8.2 %collective-permute-start = (bf16[528,384]{1,0:T(8,128)(2,1)S(1)}, bf16[528,384]{1,0:T(8,128)(2,1)S(1)}, u32[]{:S(2)}, u32[]{:S(2)}) collective-permute-start(bf16[528,384]{1,0:T(8,128)(2,1)S(1)} %pad_maximum_fusion), channel_id=1, source_target_pairs={{0,8},{8,0},{1,9},{9,1},{2,10},{10,2},{3,11},{11,3},{4,12},{12,4},... | collective-permute-start | bytes 1216520 | tf_op jit(solution)/shard_map/ppermute | solution.py:23
  117.6 42.6 %collective-permute-done = bf16[528,384]{1,0:T(8,128)(2,1)S(1)} collective-permute-done((bf16[528,384]{1,0:T(8,128)(2,1)S(1)}, bf16[528,384]{1,0:T(8,128)(2,1)S(1)}, u32[]{:S(2)}, u32[]{:S(2)}) %collective-permute-start) | collective-permute-done | bytes 405536 | tf_op jit(solution)/shard_map/ppermute | solution.py:23
  160.2 0.1 broadcast_in_dim.65
  160.3 22.9 %all_to_all.16 = bf16[4,528,384]{2,1,0:T(8,128)(2,1)} all-to-all(bf16[4,528,384]{2,1,0:T(8,128)(2,1)S(1)} %broadcast_in_dim.65), channel_id=1, replica_groups=mesh['zl'=8,'x'=4,'zh'=2,'y'=4,'c'=2] {'y'}, dimensions={0} | all-to-all | bytes 3244032 | tf_op jit(solution)/shard_map/all_to_all | solution.py:121
  183.3 10.8 %collective-permute-start.1 = (bf16[768,768]{1,0:T(8,128)(2,1)}, bf16[768,768]{1,0:T(8,128)(2,1)S(1)}, u32[]{:S(2)}, u32[]{:S(2)}) collective-permute-start(bf16[768,768]{1,0:T(8,128)(2,1)} %all-gather.7.cloned.1.call-done.refs_0_), channel_id=1, source_target_pairs={{0,16},{16,32},{32,48},{48,0},{1,17},{17,33},{33,49},{49,1},{2,18}... | collective-permute-start | bytes 3538952 | tf_op jit(solution)/shard_map/ppermute | solution.py:23
  194.1 1.9 collective-permute-start.2
  196.1 3.9 %collective-permute-start.5 = (bf16[768,768]{1,0:T(8,128)(2,1)}, bf16[768,768]{1,0:T(8,128)(2,1)S(1)}, u32[]{:S(2)}, u32[]{:S(2)}) collective-permute-start(bf16[768,768]{1,0:T(8,128)(2,1)} %all-gather.9.cloned.1.call-done.refs_5_), channel_id=1, source_target_pairs={{0,16},{16,32},{32,48},{48,0},{1,17},{17,33},{33,49},{49,1},{2,18}... | collective-permute-start | bytes 3538952 | tf_op jit(solution)/shard_map/ppermute | solution.py:23
  200.0 3.1 %collective-permute-start.6 = (bf16[768,768]{1,0:T(8,128)(2,1)}, bf16[768,768]{1,0:T(8,128)(2,1)S(1)}, u32[]{:S(2)}, u32[]{:S(2)}) collective-permute-start(bf16[768,768]{1,0:T(8,128)(2,1)} %all-gather.9.cloned.1.call-done.refs_5_), channel_id=1, source_target_pairs={{0,48},{16,0},{32,16},{48,32},{1,49},{17,1},{33,17},{49,33},{2,50}... | collective-permute-start | bytes 3538952 | tf_op jit(solution)/shard_map/ppermute | solution.py:23
  203.2 17.7 %collective-permute-done.1.refs_1_ = bf16[768,768]{1,0:T(8,128)(2,1)S(1)} collective-permute-done((bf16[768,768]{1,0:T(8,128)(2,1)}, bf16[768,768]{1,0:T(8,128)(2,1)S(1)}, u32[]{:S(2)}, u32[]{:S(2)}) %collective-permute-start.1) | collective-permute-done | bytes 1179680 | tf_op jit(solution)/shard_map/ppermute | solution.py:23
  220.9 0.9 slice.63
  221.7 4.4 %collective-permute-start.3 = (bf16[384,768]{1,0:T(8,128)(2,1)}, bf16[384,768]{1,0:T(8,128)(2,1)}, u32[]{:S(2)}, u32[]{:S(2)}) collective-permute-start(bf16[384,768]{1,0:T(8,128)(2,1)} %slice.63), channel_id=1, source_target_pairs={{0,16},{16,32},{32,48},{48,0},{1,17},{17,33},{33,49},{49,1},{2,18}... | collective-permute-start | bytes 1769480 | tf_op jit(solution)/shard_map/ppermute | solution.py:23
  226.1 0.9 slice.64
  227.0 2.8 collective-permute-start.4
  229.8 16.4 %collective-permute-done.5.refs_6_ = bf16[768,768]{1,0:T(8,128)(2,1)S(1)} collective-permute-done((bf16[768,768]{1,0:T(8,128)(2,1)}, bf16[768,768]{1,0:T(8,128)(2,1)S(1)}, u32[]{:S(2)}, u32[]{:S(2)}) %collective-permute-start.5) | collective-permute-done | bytes 1179680 | tf_op jit(solution)/shard_map/ppermute | solution.py:23
  246.1 0.8 slice.65
  247.0 1.1 copy-done.1
  248.0 4.3 %collective-permute-start.7 = (bf16[384,768]{1,0:T(8,128)(2,1)}, bf16[384,768]{1,0:T(8,128)(2,1)}, u32[]{:S(2)}, u32[]{:S(2)}) collective-permute-start(bf16[384,768]{1,0:T(8,128)(2,1)} %slice.65), channel_id=1, source_target_pairs={{0,16},{16,32},{32,48},{48,0},{1,17},{17,33},{33,49},{49,1},{2,18}... | collective-permute-start | bytes 1769480 | tf_op jit(solution)/shard_map/ppermute | solution.py:23
  252.3 0.9 slice.66
  253.2 1.0 copy-done.3
  254.2 2.8 collective-permute-start.8
  257.1 1.7 collective-permute-done.3.refs_3_
  258.8 4.4 %collective-permute-done.4.refs_4_ = bf16[384,768]{1,0:T(8,128)(2,1)} collective-permute-done((bf16[384,768]{1,0:T(8,128)(2,1)}, bf16[384,768]{1,0:T(8,128)(2,1)}, u32[]{:S(2)}, u32[]{:S(2)}) %collective-permute-start.4) | collective-permute-done | bytes 589856 | tf_op jit(solution)/shard_map/ppermute | solution.py:23
  263.2 4.9 %collective-permute-done.7.refs_8_ = bf16[384,768]{1,0:T(8,128)(2,1)} collective-permute-done((bf16[384,768]{1,0:T(8,128)(2,1)}, bf16[384,768]{1,0:T(8,128)(2,1)}, u32[]{:S(2)}, u32[]{:S(2)}) %collective-permute-start.7) | collective-permute-done | bytes 589856 | tf_op jit(solution)/shard_map/ppermute | solution.py:23
  268.1 4.1 %collective-permute-done.8.refs_9_ = bf16[384,768]{1,0:T(8,128)(2,1)} collective-permute-done((bf16[384,768]{1,0:T(8,128)(2,1)}, bf16[384,768]{1,0:T(8,128)(2,1)}, u32[]{:S(2)}, u32[]{:S(2)}) %collective-permute-start.8) | collective-permute-done | bytes 589856 | tf_op jit(solution)/shard_map/ppermute | solution.py:23
  272.2 1.3 copy-done.2
  273.5 1.3 copy-done.4
  274.7 1.3 copy-done.5
  276.0 1.3 copy-done.6
  277.3 25.6 %shard_map.64 = bf16[512,768]{1,0:T(8,128)(2,1)} custom-call(s32[2]{0:T(128)S(1)} %pad_add_fusion.place_ref, bf16[2,4,528,384]{3,2,1,0:T(8,128)(2,1)} %bitcast.63, bf16[2,4,528,384]{3,2,1,0:T(8,128)(2,1)} %bitcast.64, bf16[1,768]{1,0:T(2,128)(2,1)S(1)} %broadcast_in_dim.66.bias_ref, bf16[768,768]{1,0:T(8,128)(2,1)S(1)} %copy-done.5, ...), custom_call_target="tpu_custom_call" | custom-call | flops 4831838208 | bytes 15728640 | tf_op jit(solution)/shard_map/pallas_call | solution.py:93
  (46 shorter events, 0.8 us)
Async XLA Ops:
  6.5 3.7 %copy-start = (bf16[1024,384]{1,0:T(8,128)(2,1)S(1)}, bf16[1024,384]{1,0:T(8,128)(2,1)}, u32[]{:S(2)}) copy-start(bf16[1024,384]{1,0:T(8,128)(2,1)} %param.6) | copy-start | bytes 2359300
  6.5 176.7 %all-gather.7.cloned.1.call-start = ((), (), s32[]{:S(2)}) async-start(), calls=%async_computation.3 | async-start | bytes 1327104 | tf_op jit(solution)/shard_map/all_gather | solution.py:112
  11.0 17.1 %copy-start.7 = (s32[32,32]{1,0:T(8,128)S(1)}, s32[32,32]{1,0:T(8,128)}, u32[]{:S(2)}) copy-start(s32[32,32]{1,0:T(8,128)} %param.7) | copy-start | bytes 12292
  12.0 73.1 %all-to-all-start = ((bf16[32,32,384]{2,1,0:T(8,128)(2,1)}), bf16[32,32,384]{2,1,0:T(8,128)(2,1)S(1)}, u32[]{:S(2)}, u32[]{:S(2)}) async-start(bf16[32,32,384]{2,1,0:T(8,128)(2,1)} %broadcast_select_fusion), calls=%async_computation | async-start | bytes 1572864 | tf_op jit(solution)/shard_map/all_to_all | solution.py:135
  27.3 168.8 %all-gather.9.cloned.1.call-start = ((), (), s32[]{:S(2)}) async-start(), calls=%async_computation.4 | async-start | bytes 1327104 | tf_op jit(solution)/shard_map/all_gather | solution.py:112
  28.0 244.2 %all-gather.11.cloned.1.call-start = ((), (), s32[]{:S(2)}) async-start(), calls=%async_computation.5 | async-start | bytes 4866048 | tf_op jit(solution)/shard_map/all_gather | solution.py:122
  85.1 2.1 copy-start.9
  109.4 162.8 %all-gather.13.cloned.1.call-start = ((), (), s32[]{:S(2)}) async-start(), calls=%async_computation.6 | async-start | bytes 4866048 | tf_op jit(solution)/shard_map/all_gather | solution.py:122
  109.4 50.8 %collective-permute-start = (bf16[528,384]{1,0:T(8,128)(2,1)S(1)}, bf16[528,384]{1,0:T(8,128)(2,1)S(1)}, u32[]{:S(2)}, u32[]{:S(2)}) collective-permute-start(bf16[528,384]{1,0:T(8,128)(2,1)S(1)} %pad_maximum_fusion), channel_id=1, source_target_pairs={{0,8},{8,0},{1,9},{9,1},{2,10},{10,2},{3,11},{11,3},{4,12},{12,4},... | collective-permute-start | bytes 1216520 | tf_op jit(solution)/shard_map/ppermute | solution.py:23
  183.3 37.6 %collective-permute-start.1 = (bf16[768,768]{1,0:T(8,128)(2,1)}, bf16[768,768]{1,0:T(8,128)(2,1)S(1)}, u32[]{:S(2)}, u32[]{:S(2)}) collective-permute-start(bf16[768,768]{1,0:T(8,128)(2,1)} %all-gather.7.cloned.1.call-done.refs_0_), channel_id=1, source_target_pairs={{0,16},{16,32},{32,48},{48,0},{1,17},{17,33},{33,49},{49,1},{2,18}... | collective-permute-start | bytes 3538952 | tf_op jit(solution)/shard_map/ppermute | solution.py:23
  194.1 32.0 %collective-permute-start.2 = (bf16[768,768]{1,0:T(8,128)(2,1)}, bf16[768,768]{1,0:T(8,128)(2,1)S(1)}, u32[]{:S(2)}, u32[]{:S(2)}) collective-permute-start(bf16[768,768]{1,0:T(8,128)(2,1)} %all-gather.7.cloned.1.call-done.refs_0_), channel_id=1, source_target_pairs={{0,48},{16,0},{32,16},{48,32},{1,49},{17,1},{33,17},{49,33},{2,50}... | collective-permute-start | bytes 3538952 | tf_op jit(solution)/shard_map/ppermute | solution.py:23
  196.1 50.0 %collective-permute-start.5 = (bf16[768,768]{1,0:T(8,128)(2,1)}, bf16[768,768]{1,0:T(8,128)(2,1)S(1)}, u32[]{:S(2)}, u32[]{:S(2)}) collective-permute-start(bf16[768,768]{1,0:T(8,128)(2,1)} %all-gather.9.cloned.1.call-done.refs_5_), channel_id=1, source_target_pairs={{0,16},{16,32},{32,48},{48,0},{1,17},{17,33},{33,49},{49,1},{2,18}... | collective-permute-start | bytes 3538952 | tf_op jit(solution)/shard_map/ppermute | solution.py:23
  200.0 52.3 %collective-permute-start.6 = (bf16[768,768]{1,0:T(8,128)(2,1)}, bf16[768,768]{1,0:T(8,128)(2,1)S(1)}, u32[]{:S(2)}, u32[]{:S(2)}) collective-permute-start(bf16[768,768]{1,0:T(8,128)(2,1)} %all-gather.9.cloned.1.call-done.refs_5_), channel_id=1, source_target_pairs={{0,48},{16,0},{32,16},{48,32},{1,49},{17,1},{33,17},{49,33},{2,50}... | collective-permute-start | bytes 3538952 | tf_op jit(solution)/shard_map/ppermute | solution.py:23
  221.7 35.3 %copy-start.8 = (bf16[768]{0:T(1024)(128)(2,1)S(1)}, bf16[768]{0:T(1024)(128)(2,1)}, u32[]{:S(2)}) copy-start(bf16[768]{0:T(1024)(128)(2,1)} %param.11) | copy-start | bytes 4612
  221.7 37.1 %collective-permute-start.3 = (bf16[384,768]{1,0:T(8,128)(2,1)}, bf16[384,768]{1,0:T(8,128)(2,1)}, u32[]{:S(2)}, u32[]{:S(2)}) collective-permute-start(bf16[384,768]{1,0:T(8,128)(2,1)} %slice.63), channel_id=1, source_target_pairs={{0,16},{16,32},{32,48},{48,0},{1,17},{17,33},{33,49},{49,1},{2,18}... | collective-permute-start | bytes 1769480 | tf_op jit(solution)/shard_map/ppermute | solution.py:23
  227.0 36.2 %collective-permute-start.4 = (bf16[384,768]{1,0:T(8,128)(2,1)}, bf16[384,768]{1,0:T(8,128)(2,1)}, u32[]{:S(2)}, u32[]{:S(2)}) collective-permute-start(bf16[384,768]{1,0:T(8,128)(2,1)} %slice.64), channel_id=1, source_target_pairs={{0,48},{16,0},{32,16},{48,32},{1,49},{17,1},{33,17},{49,33},{2,50}... | collective-permute-start | bytes 1769480 | tf_op jit(solution)/shard_map/ppermute | solution.py:23
  247.0 1.1 copy-start.1
  248.0 20.0 %collective-permute-start.7 = (bf16[384,768]{1,0:T(8,128)(2,1)}, bf16[384,768]{1,0:T(8,128)(2,1)}, u32[]{:S(2)}, u32[]{:S(2)}) collective-permute-start(bf16[384,768]{1,0:T(8,128)(2,1)} %slice.65), channel_id=1, source_target_pairs={{0,16},{16,32},{32,48},{48,0},{1,17},{17,33},{33,49},{49,1},{2,18}... | collective-permute-start | bytes 1769480 | tf_op jit(solution)/shard_map/ppermute | solution.py:23
  253.2 1.0 copy-start.3
  254.2 17.9 %collective-permute-start.8 = (bf16[384,768]{1,0:T(8,128)(2,1)}, bf16[384,768]{1,0:T(8,128)(2,1)}, u32[]{:S(2)}, u32[]{:S(2)}) collective-permute-start(bf16[384,768]{1,0:T(8,128)(2,1)} %slice.66), channel_id=1, source_target_pairs={{0,48},{16,0},{32,16},{48,32},{1,49},{17,1},{33,17},{49,33},{2,50}... | collective-permute-start | bytes 1769480 | tf_op jit(solution)/shard_map/ppermute | solution.py:23
  272.2 1.3 copy-start.2
  273.5 1.3 copy-start.4
  274.7 1.3 copy-start.5
  276.0 1.3 copy-start.6
Sparse Core Ops, SparseCore 0:
  9.4 80.0 all-gather.6
  91.6 82.0 all-gather.8
  175.8 25.1 all-gather.10
  203.0 24.0 all-gather.12

commit v2 on v1

v2 whole, which is shorter than its diff:
```python
import functools

import jax
import jax.numpy as jnp
from jax import lax
from jax.experimental import pallas as pl
from jax.experimental.pallas import tpu as pltpu
from jax.sharding import Mesh, PartitionSpec as P

D = 6144
RECV = 512
PART = 384
BLOCK = 192
COLS = 768
GAIN_ROWS = 16
ROWS = RECV + GAIN_ROWS
STRIP = 32
INV_SQRT2 = 0.7071067811865476


def shift(value, axis, size, step):
    return lax.ppermute(value, axis, [(i, (i + step) % size) for i in range(size)])


def row_copies(place_ref, pieces, w_all, sems):
    own, below, above, far_a, far_b = pieces
    x = place_ref[0]
    copies = []
    for z in range(8):
        far = far_a if z < 4 else far_b
        for ref, at, step in ((own, z, 0), (below, z, 3), (above, z, 1), (far, z % 4, 2)):
            block = 4 * z + lax.rem(x + step, 4)
            copies.append(
                pltpu.make_async_copy(
                    ref.at[pl.ds(at * BLOCK, BLOCK), :],
                    w_all.at[pl.ds(pl.multiple_of(block * BLOCK, 64), BLOCK), :],
                    sems.at[len(copies)],
                )
            )
    return copies


def mlp_kernel(place_ref, *refs):
    rows_refs, bias_ref, pieces = refs[:2], refs[2], refs[3:8]
    out_ref, w_all, normed, sems = refs[8:]
    half = place_ref[1]
    copies = row_copies(place_ref, pieces, w_all, sems)
    for copy in copies:
        copy.start()

    chunks = [
        (rows_refs[side], part, 8 * lax.rem(half + side, 2) + part)
        for side in range(2)
        for part in range(8)
    ]

    @pl.loop(0, RECV // STRIP)
    def _(strip):
        rows = pl.ds(pl.multiple_of(strip * STRIP, STRIP), STRIP)
        total = jnp.zeros((STRIP, 128), jnp.float32)
        square = jnp.zeros((STRIP, 128), jnp.float32)
        for ref, part, _at in chunks:
            for lane in range(PART // 128):
                v = ref[part, rows, lane * 128 : (lane + 1) * 128].astype(jnp.float32)
                total += v
                square += v * v
        row_mean = jnp.sum(total, axis=1, keepdims=True) / D
        variance = jnp.sum(square, axis=1, keepdims=True) / D - row_mean * row_mean
        scale = lax.rsqrt(variance + 1e-06)
        for ref, part, at in chunks:
            v = ref[part, rows, :].astype(jnp.float32)
            gain = ref[part, RECV : RECV + 1, :].astype(jnp.float32)
            columns = pl.ds(pl.multiple_of(at * PART, 128), PART)
            normed[rows, columns] = ((v - row_mean) * scale * gain).astype(jnp.bfloat16)

    for copy in copies:
        copy.wait()
    for n in range(COLS // 256):
        cols = slice(n * 256, (n + 1) * 256)
        v = jnp.dot(normed[...], w_all[:, cols], preferred_element_type=jnp.float32)
        v = v + bias_ref[:, cols].astype(jnp.float32)
        out_ref[:, cols] = (v * (1.0 + lax.erf(v * INV_SQRT2)) * 0.5).astype(jnp.bfloat16)


def mlp(place, rows, bias, pieces):
    vmem = pl.BlockSpec(memory_space=pltpu.VMEM)
    return pl.pallas_call(
        mlp_kernel,
        out_shape=jax.ShapeDtypeStruct((RECV, COLS), jnp.bfloat16),
        in_specs=[pl.BlockSpec(memory_space=pltpu.SMEM)]
        + [vmem] * 3
        + [pl.BlockSpec(memory_space=pl.ANY)] * len(pieces),
        out_specs=vmem,
        scratch_shapes=[
            pltpu.VMEM((D, COLS), jnp.bfloat16),
            pltpu.VMEM((RECV, D), jnp.bfloat16),
            pltpu.SemaphoreType.DMA((32,)),
        ],
        compiler_params=pltpu.CompilerParams(vmem_limit_bytes=26 * 1024 * 1024),
        cost_estimate=pl.CostEstimate(
            flops=2 * RECV * D * COLS, bytes_accessed=2 * (RECV * D + D * COLS), transcendentals=RECV * COLS
        ),
    )(place, *rows, bias, *pieces)


def beside(own):
    return [shift(own, "x", 4, 1), shift(own, "x", 4, -1)]


def across(below, above):
    middle = below.shape[0] // 2
    return [shift(below[:middle], "x", 4, 1), shift(above[middle:], "x", 4, -1)]


def together(*lists):
    return lax.optimization_barrier(tuple(lists))


def local(x_tiles, counts, owners, ln_gain, w_up, up_bias):
    own = lax.all_gather(w_up, "zl", axis=0, tiled=True)
    near = beside(own)
    far = across(*near)

    groups = 32
    my_index = lax.axis_index(("zl", "x"))
    slots = x_tiles.shape[0] // groups
    tile_block = x_tiles.reshape(groups, slots, PART)
    inverse = jnp.argsort(owners, axis=1)
    my_tiles = lax.dynamic_index_in_dim(inverse, my_index, 0, keepdims=False)
    outgoing = jnp.take(tile_block, my_tiles, axis=0)
    source_tiles = lax.dynamic_index_in_dim(inverse, my_index, 1, keepdims=False)
    held_rows = jnp.take_along_axis(counts, source_tiles[:, None], axis=1)[:, 0]
    inclusive = jnp.cumsum(held_rows)
    exclusive = inclusive - held_rows
    positions = jnp.arange(RECV, dtype=jnp.int32)
    source = jnp.sum((inclusive[None, :] <= positions[:, None]).astype(jnp.int32), axis=1)
    slot_index = positions - jnp.take(exclusive, source)
    flat_index = source * slots + slot_index
    outgoing, flat_index = together(outgoing, flat_index)
    incoming = lax.all_to_all(outgoing, ("zl", "x"), split_axis=0, concat_axis=0, tiled=True)
    packed = jnp.take(incoming.reshape(groups * slots, PART), flat_index, axis=0)

    gains = jnp.broadcast_to(ln_gain[None, :], (GAIN_ROWS, PART))
    mine = jnp.concatenate([packed, gains], axis=0)
    other = shift(mine, "zh", 2, 1)
    other, near = together(other, near)
    pieces = [own, *near, *far]
    rows = [lax.all_gather(part, ("y", "c"), axis=0) for part in (mine, other)]
    axes = [lax.axis_index(axis) for axis in ("x", "zh")]
    return mlp(jnp.stack(axes).astype(jnp.int32), rows, up_bias[None, :], pieces)


def solution(mesh):
    fine = Mesh(mesh.devices.reshape(8, 4, 2, 4, 2), ("zl", "x", "zh", "y", "c"))
    dp, mp = ("zl", "x"), ("zh", "y", "c")
    return jax.shard_map(
        local,
        mesh=fine,
        in_specs=(P(dp, mp), P(), P(), P(mp), P(dp, mp), P(mp)),
        out_specs=P(dp, mp),
        check_vma=False,
    )
```

time: 310 us -> 233 us (0.75)
  the two profiles are of different devices: /device:TPU:32 before, /device:TPU:1 now
where the time goes in v2:
time: 233 us; the launch traced here: 232 us
  waiting for transfers between devices  129 us (55%)
  starting transfers between devices  37.1 us (16%)
  other arithmetic  23.4 us (10%)
  local copies, waits for them, and re-layouts  15.6 us (7%)
  between operations  13.4 us (6%)
  Pallas kernels  12.8 us (5%)
    ppermute x5, waiting for transfers between devices, shift(): lax.ppermute(value, axis, [(i, (i + step) % size) for i in range(size)])  64.7 us
    all_to_all x1, waiting for transfers between devices, local(): lax.all_to_all(outgoing, ('zl', 'x'), split_axis=0, concat_axis=0, tiled=...  61.2 us
    ppermute x5, starting transfers between devices, shift(): lax.ppermute(value, axis, [(i, (i + step) % size) for i in range(size)])  21.1 us
    all_to_all x1, starting transfers between devices, local(): lax.all_to_all(outgoing, ('zl', 'x'), split_axis=0, concat_axis=0, tiled=...  15.9 us
    add x1, other arithmetic, local(): flat_index = source * slots + slot_index  15.7 us
    pallas_call x1, Pallas kernels, mlp(): pl.pallas_call(mlp_kernel, out_shape=jax.ShapeDtypeStruct((RECV, COLS), j...  12.8 us
    unnamed x16, local copies, waits for them, and re-layouts  6.31 us
  transfers between devices with their start and end apart: 9, of which 7 were waited for; matrix products, arithmetic and copies ran while one was open for 14% of the time, Pallas kernels for 0%

profile of v2, /device:TPU:1, one launch (start us, length us, event | category | flops | bytes accessed | tf_op | source)
XLA Modules:
  0.0 231.5 jit_solution(15175861369461438893)
XLA Ops:
  6.5 0.0 copy-start
  6.5 0.7 all-gather.6.cloned.1.call-update
  7.3 0.8 copy.10
  8.1 0.8 sort.17
  8.9 0.2 dynamic-slice_reduce_fusion
  9.1 1.5 gather_fusion.2
  10.6 0.1 copy.11
  10.7 0.1 reduce-window.8
  10.7 0.1 reduce.2
  10.9 0.1 convert_reduce_fusion
  10.9 0.7 fusion.5
  11.7 0.7 fusion.4
  12.4 4.3 %compare_select_fusion.1 = (s32[512,1]{0,1:T(1,128)S(1)}, s32[512,1]{0,1:T(1,128)S(1)}) fusion(s32[]{:T(128)} %bitcast.35, s32[]{:T(128)} %bitcast.36, s32[]{:T(128)} %bitcast.37, s32[]{:T(128)} %bitcast.38, s32[]{:T(128)} %bitcast.39, s32[]{:T(128)} %bitcast.41, s32[]{:T(128)} %bitcast.40, s32[512,1]{0,1:T(1,128)S(1)} %bitcast.58), kind=kLoop, calls=%fused_computation.35 | loop fusion | flops 7680 | bytes 6172 | tf_op jit(solution)/shard_map/jit(_take)/gather | solution.py:137
  16.7 0.2 compare_reduce_fusion.24
  16.9 0.0 copy-done
  16.9 0.7 gather_fusion
  17.7 15.7 %fusion.1 = s32[512]{0:T(512)S(1)} fusion(pred[512]{0:T(512)(128)(4,1)S(1)} %get-tuple-element.41, pred[512]{0:T(512)(128)(4,1)S(1)} %get-tuple-element.40, pred[512]{0:T(512)(128)(4,1)S(1)} %get-tuple-element.39, pred[512]{0:T(512)(128)(4,1)S(1)} %get-tuple-element.38, pred[512]{0:T(512)(128)(4,1)S(1)} %get-tuple-element.37, ...), kind=kLoop, calls=%fused_computation.50 | loop fusion | flops 17920 | bytes 19044 | tf_op jit(solution)/shard_map/add | solution.py:138
  33.4 1.0 broadcast_select_fusion
  34.5 15.9 %all-to-all-start = ((bf16[32,32,384]{2,1,0:T(8,128)(2,1)}), bf16[32,32,384]{2,1,0:T(8,128)(2,1)S(1)}, u32[]{:S(2)}, u32[]{:S(2)}) async-start(bf16[32,32,384]{2,1,0:T(8,128)(2,1)} %broadcast_select_fusion), calls=%async_computation | async-start | bytes 1572864 | tf_op jit(solution)/shard_map/all_to_all | solution.py:140
  50.4 0.0 copy-start.6
  50.4 0.0 all-gather.8.cloned.1.call-start
  50.5 61.2 %all-to-all-done = bf16[32,32,384]{2,1,0:T(8,128)(2,1)S(1)} async-done(((bf16[32,32,384]{2,1,0:T(8,128)(2,1)}), bf16[32,32,384]{2,1,0:T(8,128)(2,1)S(1)}, u32[]{:S(2)}, u32[]{:S(2)}) %all-to-all-start) | async-done | bytes 786464 | tf_op jit(solution)/shard_map/all_to_all | solution.py:140
  111.7 1.9 gather_fusion.1
  113.7 0.1 broadcast_select_fusion.1
  113.8 0.8 pad_maximum_fusion
  114.6 0.0 all-gather.8.cloned.1.call-update
  114.7 0.0 all-gather.10.cloned.1.call-start
  114.7 0.0 all-gather.6.cloned.1.call-done.refs_3_
  114.7 3.1 %collective-permute-start.1 = (bf16[1536,768]{1,0:T(8,128)(2,1)}, bf16[1536,768]{1,0:T(8,128)(2,1)S(1)}, u32[]{:S(2)}, u32[]{:S(2)}) collective-permute-start(bf16[1536,768]{1,0:T(8,128)(2,1)} %all-gather.6.cloned.1.call-done.refs_3_), channel_id=1, source_target_pairs={{0,16},{16,32},{32,48},{48,0},{1,17},{17,33},{33,49},{49,1},{2,18}... | collective-permute-start | bytes 7077896 | tf_op jit(solution)/shard_map/ppermute | solution.py:22
  117.8 3.4 %collective-permute-start.2 = (bf16[1536,768]{1,0:T(8,128)(2,1)}, bf16[1536,768]{1,0:T(8,128)(2,1)}, u32[]{:S(2)}, u32[]{:S(2)}) collective-permute-start(bf16[1536,768]{1,0:T(8,128)(2,1)} %all-gather.6.cloned.1.call-done.refs_3_), channel_id=1, source_target_pairs={{0,48},{16,0},{32,16},{48,32},{1,49},{17,1},{33,17},{49,33},{2,50}... | collective-permute-start | bytes 7077896 | tf_op jit(solution)/shard_map/ppermute | solution.py:22
  121.2 8.1 %collective-permute-start = (bf16[528,384]{1,0:T(8,128)(2,1)}, bf16[528,384]{1,0:T(8,128)(2,1)S(1)}, u32[]{:S(2)}, u32[]{:S(2)}) collective-permute-start(bf16[528,384]{1,0:T(8,128)(2,1)} %pad_maximum_fusion), channel_id=1, source_target_pairs={{0,8},{8,0},{1,9},{9,1},{2,10},{10,2},{3,11},{11,3},{4,12},{12,4},... | collective-permute-start | bytes 1216520 | tf_op jit(solution)/shard_map/ppermute | solution.py:22
  129.4 33.8 %collective-permute-done = bf16[528,384]{1,0:T(8,128)(2,1)S(1)} collective-permute-done((bf16[528,384]{1,0:T(8,128)(2,1)}, bf16[528,384]{1,0:T(8,128)(2,1)S(1)}, u32[]{:S(2)}, u32[]{:S(2)}) %collective-permute-start) | collective-permute-done | bytes 405536 | tf_op jit(solution)/shard_map/ppermute | solution.py:22
  163.2 6.0 %collective-permute-done.1.refs_4_ = bf16[1536,768]{1,0:T(8,128)(2,1)S(1)} collective-permute-done((bf16[1536,768]{1,0:T(8,128)(2,1)}, bf16[1536,768]{1,0:T(8,128)(2,1)S(1)}, u32[]{:S(2)}, u32[]{:S(2)}) %collective-permute-start.1) | collective-permute-done | bytes 2359328 | tf_op jit(solution)/shard_map/ppermute | solution.py:22
  169.1 1.7 collective-permute-done.2.refs_5_
  170.9 0.0 all-gather.10.cloned.1.call-update
  170.9 0.0 copy-start.5
  170.9 1.1 slice.47
  172.0 3.2 %collective-permute-start.3 = (bf16[768,768]{1,0:T(8,128)(2,1)}, bf16[768,768]{1,0:T(8,128)(2,1)}, u32[]{:S(2)}, u32[]{:S(2)}) collective-permute-start(bf16[768,768]{1,0:T(8,128)(2,1)} %slice.47), channel_id=1, source_target_pairs={{0,16},{16,32},{32,48},{48,0},{1,17},{17,33},{33,49},{49,1},{2,18}... | collective-permute-start | bytes 3538952 | tf_op jit(solution)/shard_map/ppermute | solution.py:22
  175.2 2.4 %slice.48 = bf16[768,768]{1,0:T(8,128)(2,1)} slice(bf16[1536,768]{1,0:T(8,128)(2,1)} %collective-permute-done.2.refs_5_), slice={[768:1536], [0:768]} | slice | bytes 2359296 | tf_op jit(solution)/shard_map/slice | solution.py:112
  177.5 3.3 %collective-permute-start.4 = (bf16[768,768]{1,0:T(8,128)(2,1)}, bf16[768,768]{1,0:T(8,128)(2,1)}, u32[]{:S(2)}, u32[]{:S(2)}) collective-permute-start(bf16[768,768]{1,0:T(8,128)(2,1)} %slice.48), channel_id=1, source_target_pairs={{0,48},{16,0},{32,16},{48,32},{1,49},{17,1},{33,17},{49,33},{2,50}... | collective-permute-start | bytes 3538952 | tf_op jit(solution)/shard_map/ppermute | solution.py:22
  180.9 0.1 pad_add_fusion.place_ref
  181.0 19.1 %collective-permute-done.3.refs_6_ = bf16[768,768]{1,0:T(8,128)(2,1)} collective-permute-done((bf16[768,768]{1,0:T(8,128)(2,1)}, bf16[768,768]{1,0:T(8,128)(2,1)}, u32[]{:S(2)}, u32[]{:S(2)}) %collective-permute-start.3) | collective-permute-done | bytes 1179680 | tf_op jit(solution)/shard_map/ppermute | solution.py:22
  200.1 4.1 %collective-permute-done.4.refs_7_ = bf16[768,768]{1,0:T(8,128)(2,1)} collective-permute-done((bf16[768,768]{1,0:T(8,128)(2,1)}, bf16[768,768]{1,0:T(8,128)(2,1)}, u32[]{:S(2)}, u32[]{:S(2)}) %collective-permute-start.4) | collective-permute-done | bytes 1179680 | tf_op jit(solution)/shard_map/ppermute | solution.py:22
  204.1 2.5 %all-gather.10.cloned.1.call-done = bf16[4224,384]{1,0:T(8,128)(2,1)} async-done(((bf16[528,384]{1,0:T(8,128)(2,1)}), bf16[4224,384]{1,0:T(8,128)(2,1)}) %all-gather.10.cloned.1.call-update) | async-done | bytes 3244048 | tf_op jit(solution)/shard_map/all_gather | solution.py:148
  206.6 1.9 copy-done.1
  208.5 1.9 copy-done.2
  210.5 1.7 copy-done.3
  212.1 12.8 %shard_map.64 = bf16[512,768]{1,0:T(8,128)(2,1)} custom-call(s32[2]{0:T(128)S(1)} %pad_add_fusion.place_ref, bf16[8,528,384]{2,1,0:T(8,128)(2,1)S(1)} %bitcast.55, bf16[8,528,384]{2,1,0:T(8,128)(2,1)S(1)} %bitcast.56, bf16[1,768]{1,0:T(2,128)(2,1)S(1)} %broadcast_in_dim.52.refs_2_, bf16[1536,768]{1,0:T(8,128)(2,1)S(1)} %copy-done.3, ...), custom_call_target="tpu_custom_call" | custom-call | flops 4831838208 | bytes 15728640 | tf_op jit(solution)/shard_map/pallas_call | solution.py:87
  (23 shorter events, 0.1 us)
Async XLA Ops:
  6.5 10.4 %copy-start = (bf16[1024,384]{1,0:T(8,128)(2,1)S(1)}, bf16[1024,384]{1,0:T(8,128)(2,1)}, u32[]{:S(2)}) copy-start(bf16[1024,384]{1,0:T(8,128)(2,1)} %param.6) | copy-start | bytes 2359300
  6.5 108.2 %all-gather.6.cloned.1.call-start = ((), (), s32[]{:S(2)}) async-start(), calls=%async_computation.1 | async-start | bytes 2654208 | tf_op jit(solution)/shard_map/all_gather | solution.py:120
  34.5 77.3 %all-to-all-start = ((bf16[32,32,384]{2,1,0:T(8,128)(2,1)}), bf16[32,32,384]{2,1,0:T(8,128)(2,1)S(1)}, u32[]{:S(2)}, u32[]{:S(2)}) async-start(bf16[32,32,384]{2,1,0:T(8,128)(2,1)} %broadcast_select_fusion), calls=%async_computation | async-start | bytes 1572864 | tf_op jit(solution)/shard_map/all_to_all | solution.py:140
  50.4 63.4 %copy-start.6 = (bf16[384]{0:T(512)(128)(2,1)S(1)}, bf16[384]{0:T(512)(128)(2,1)}, u32[]{:S(2)}) copy-start(bf16[384]{0:T(512)(128)(2,1)} %param.9) | copy-start | bytes 2308
  50.4 153.7 %all-gather.8.cloned.1.call-start = ((), (), s32[]{:S(2)}) async-start(), calls=%async_computation.2 | async-start | bytes 3649536 | tf_op jit(solution)/shard_map/all_gather | solution.py:148
  114.7 92.0 %all-gather.10.cloned.1.call-start = ((), (), s32[]{:S(2)}) async-start(), calls=%async_computation.3 | async-start | bytes 3649536 | tf_op jit(solution)/shard_map/all_gather | solution.py:148
  114.7 54.4 %collective-permute-start.1 = (bf16[1536,768]{1,0:T(8,128)(2,1)}, bf16[1536,768]{1,0:T(8,128)(2,1)S(1)}, u32[]{:S(2)}, u32[]{:S(2)}) collective-permute-start(bf16[1536,768]{1,0:T(8,128)(2,1)} %all-gather.6.cloned.1.call-done.refs_3_), channel_id=1, source_target_pairs={{0,16},{16,32},{32,48},{48,0},{1,17},{17,33},{33,49},{49,1},{2,18}... | collective-permute-start | bytes 7077896 | tf_op jit(solution)/shard_map/ppermute | solution.py:22
  117.8 53.0 %collective-permute-start.2 = (bf16[1536,768]{1,0:T(8,128)(2,1)}, bf16[1536,768]{1,0:T(8,128)(2,1)}, u32[]{:S(2)}, u32[]{:S(2)}) collective-permute-start(bf16[1536,768]{1,0:T(8,128)(2,1)} %all-gather.6.cloned.1.call-done.refs_3_), channel_id=1, source_target_pairs={{0,48},{16,0},{32,16},{48,32},{1,49},{17,1},{33,17},{49,33},{2,50}... | collective-permute-start | bytes 7077896 | tf_op jit(solution)/shard_map/ppermute | solution.py:22
  121.2 41.9 %collective-permute-start = (bf16[528,384]{1,0:T(8,128)(2,1)}, bf16[528,384]{1,0:T(8,128)(2,1)S(1)}, u32[]{:S(2)}, u32[]{:S(2)}) collective-permute-start(bf16[528,384]{1,0:T(8,128)(2,1)} %pad_maximum_fusion), channel_id=1, source_target_pairs={{0,8},{8,0},{1,9},{9,1},{2,10},{10,2},{3,11},{11,3},{4,12},{12,4},... | collective-permute-start | bytes 1216520 | tf_op jit(solution)/shard_map/ppermute | solution.py:22
  163.2 7.7 %copy-start.4 = (bf16[528,384]{1,0:T(8,128)(2,1)}, bf16[528,384]{1,0:T(8,128)(2,1)S(1)}, u32[]{:S(2)}) copy-start(bf16[528,384]{1,0:T(8,128)(2,1)S(1)} %collective-permute-done) | copy-start | bytes 1216516
  170.9 10.0 %copy-start.5 = (bf16[768]{0:T(1024)(128)(2,1)S(1)}, bf16[768]{0:T(1024)(128)(2,1)}, u32[]{:S(2)}) copy-start(bf16[768]{0:T(1024)(128)(2,1)} %param.11) | copy-start | bytes 4612
  172.0 28.1 %collective-permute-start.3 = (bf16[768,768]{1,0:T(8,128)(2,1)}, bf16[768,768]{1,0:T(8,128)(2,1)}, u32[]{:S(2)}, u32[]{:S(2)}) collective-permute-start(bf16[768,768]{1,0:T(8,128)(2,1)} %slice.47), channel_id=1, source_target_pairs={{0,16},{16,32},{32,48},{48,0},{1,17},{17,33},{33,49},{49,1},{2,18}... | collective-permute-start | bytes 3538952 | tf_op jit(solution)/shard_map/ppermute | solution.py:22
  177.5 26.6 %collective-permute-start.4 = (bf16[768,768]{1,0:T(8,128)(2,1)}, bf16[768,768]{1,0:T(8,128)(2,1)}, u32[]{:S(2)}, u32[]{:S(2)}) collective-permute-start(bf16[768,768]{1,0:T(8,128)(2,1)} %slice.48), channel_id=1, source_target_pairs={{0,48},{16,0},{32,16},{48,32},{1,49},{17,1},{33,17},{49,33},{2,50}... | collective-permute-start | bytes 3538952 | tf_op jit(solution)/shard_map/ppermute | solution.py:22
  206.6 1.9 copy-start.1
  208.5 1.9 copy-start.2
  210.5 1.7 copy-start.3
Sparse Core Ops, SparseCore 0:
  9.4 88.7 all-gather.5
  114.8 35.1 all-gather.7
  171.0 35.5 all-gather.9

commit v3 on v2

v3 whole, which is shorter than its diff:
```python
import functools

import jax
import jax.numpy as jnp
from jax import lax
from jax.experimental import pallas as pl
from jax.experimental.pallas import tpu as pltpu
from jax.sharding import Mesh, PartitionSpec as P

D = 6144
RECV = 512
PART = 384
BLOCK = 192
COLS = 768
GAIN_ROWS = 16
ROWS = RECV + GAIN_ROWS
STRIP = 32
VMEM_MIB = 60
INV_SQRT2 = 0.7071067811865476


def shift(value, axis, size, step):
    return lax.ppermute(value, axis, [(i, (i + step) % size) for i in range(size)])


def row_copies(place_ref, pieces, w_ref, sems):
    here, own, below, above, far_a, far_b = pieces
    x, z_lo = place_ref[0], place_ref[2]

    def block(at, count):
        return pl.ds(pl.multiple_of(at * BLOCK, 64), count * BLOCK)

    copies = [pltpu.make_async_copy(here, w_ref.at[block(4 * z_lo, 4), :], sems.at[28])]
    for slot in range(7):
        at = jnp.where(z_lo == slot, 7, slot)
        far = far_a if slot < 4 else far_b
        for ref, row, step in ((own, slot, 0), (below, slot, 3), (above, slot, 1), (far, slot % 4, 2)):
            copies.append(
                pltpu.make_async_copy(
                    ref.at[pl.ds(row * BLOCK, BLOCK), :],
                    w_ref.at[block(4 * at + lax.rem(x + step, 4), 1), :],
                    sems.at[len(copies) - 1],
                )
            )
    return copies


def mlp_kernel(place_ref, near_ref, far_ref, bias_ref, *refs):
    pieces, (out_ref, rows_ref, w_ref, normed_ref, row_sems, sems) = refs[:6], refs[6:]
    half = place_ref[1]
    inward = [
        pltpu.make_async_copy(ref, rows_ref.at[pl.ds(8 * side, 8)], row_sems.at[side])
        for side, ref in enumerate((near_ref, far_ref))
    ]
    copies = row_copies(place_ref, pieces, w_ref, sems)
    for copy in inward + copies:
        copy.start()
    for copy in inward:
        copy.wait()

    @pl.loop(0, RECV // STRIP)
    def _(strip):
        rows = pl.ds(pl.multiple_of(strip * STRIP, STRIP), STRIP)
        total = jnp.zeros((STRIP, 128), jnp.float32)
        square = jnp.zeros((STRIP, 128), jnp.float32)
        for index in range(16):
            for lane in range(PART // 128):
                v = rows_ref[index, rows, lane * 128 : (lane + 1) * 128].astype(jnp.float32)
                total += v
                square += v * v
        row_mean = jnp.sum(total, axis=1, keepdims=True) / D
        variance = jnp.sum(square, axis=1, keepdims=True) / D - row_mean * row_mean
        scale = lax.rsqrt(variance + 1e-06)
        for index in range(16):
            v = rows_ref[index, rows, :].astype(jnp.float32)
            gain = rows_ref[index, RECV : RECV + 1, :].astype(jnp.float32)
            at = 8 * lax.rem(half + index // 8, 2) + index % 8
            columns = pl.ds(pl.multiple_of(at * PART, 128), PART)
            normed_ref[rows, columns] = ((v - row_mean) * scale * gain).astype(jnp.bfloat16)

    for copy in copies:
        copy.wait()
    for n in range(COLS // 256):
        cols = slice(n * 256, (n + 1) * 256)
        v = jnp.dot(normed_ref[...], w_ref[:, cols], preferred_element_type=jnp.float32)
        v = v + bias_ref[:, cols].astype(jnp.float32)
        out_ref[:, cols] = (v * (1.0 + lax.erf(v * INV_SQRT2)) * 0.5).astype(jnp.bfloat16)


def mlp(place, rows, bias, pieces):
    vmem = pl.BlockSpec(memory_space=pltpu.VMEM)
    left = pl.BlockSpec(memory_space=pl.ANY)
    return pl.pallas_call(
        mlp_kernel,
        out_shape=jax.ShapeDtypeStruct((RECV, COLS), jnp.bfloat16),
        in_specs=[pl.BlockSpec(memory_space=pltpu.SMEM)] + [left] * 2 + [vmem] + [left] * 6,
        out_specs=vmem,
        scratch_shapes=[
            pltpu.VMEM((16, ROWS, PART), jnp.bfloat16),
            pltpu.VMEM((D, COLS), jnp.bfloat16),
            pltpu.VMEM((RECV, D), jnp.bfloat16),
            pltpu.SemaphoreType.DMA((2,)),
            pltpu.SemaphoreType.DMA((29,)),
        ],
        compiler_params=pltpu.CompilerParams(vmem_limit_bytes=VMEM_MIB * 1024 * 1024),
        cost_estimate=pl.CostEstimate(
            flops=2 * RECV * D * COLS, bytes_accessed=2 * (RECV * D + D * COLS), transcendentals=RECV * COLS
        ),
    )(place, *rows, bias, *pieces)


def beside(own):
    return [shift(own, "x", 4, 1), shift(own, "x", 4, -1)]


def across(below, above):
    middle = 4 * BLOCK
    return [shift(below[:middle], "x", 4, 1), shift(above[middle:], "x", 4, -1)]


def together(*lists):
    return lax.optimization_barrier(tuple(lists))


def local(x_tiles, counts, owners, ln_gain, w_up, up_bias):
    z_lo = lax.axis_index("zl")
    copies = jnp.broadcast_to(w_up[None], (4, BLOCK, COLS))
    here = lax.all_to_all(copies, "x", split_axis=0, concat_axis=0, tiled=True).reshape(4 * BLOCK, COLS)
    own = lax.all_gather(w_up, "zl", axis=0, tiled=True)
    own = lax.dynamic_update_slice(own, own[7 * BLOCK :], (z_lo * BLOCK, 0))[: 7 * BLOCK]
    near = beside(own)
    far = across(*near)

    groups = 32
    my_index = lax.axis_index(("zl", "x"))
    slots = x_tiles.shape[0] // groups
    tile_block = x_tiles.reshape(groups, slots, PART)
    inverse = jnp.argsort(owners, axis=1)
    my_tiles = lax.dynamic_index_in_dim(inverse, my_index, 0, keepdims=False)
    outgoing = jnp.take(tile_block, my_tiles, axis=0)
    source_tiles = lax.dynamic_index_in_dim(inverse, my_index, 1, keepdims=False)
    held_rows = jnp.take_along_axis(counts, source_tiles[:, None], axis=1)[:, 0]
    inclusive = jnp.cumsum(held_rows)
    exclusive = inclusive - held_rows
    positions = jnp.arange(RECV, dtype=jnp.int32)
    source = jnp.sum((inclusive[None, :] <= positions[:, None]).astype(jnp.int32), axis=1)
    chosen = source[:, None] == jnp.arange(groups, dtype=jnp.int32)[None, :]
    slot_index = positions - jnp.sum(jnp.where(chosen, exclusive[None, :], 0), axis=1)
    flat_index = source * slots + slot_index
    outgoing, flat_index, here = together(outgoing, flat_index, here)
    incoming = lax.all_to_all(outgoing, ("zl", "x"), split_axis=0, concat_axis=0, tiled=True)
    packed = jnp.take(incoming.reshape(groups * slots, PART), flat_index, axis=0)

    gains = jnp.broadcast_to(ln_gain[None, :], (GAIN_ROWS, PART))
    mine = jnp.concatenate([packed, gains], axis=0)
    other = shift(mine, "zh", 2, 1)
    other, near = together(other, near)
    pieces = [here, own, *near, *far]
    rows = [lax.all_gather(part, ("y", "c"), axis=0) for part in (mine, other)]
    axes = [lax.axis_index(axis) for axis in ("x", "zh", "zl")]
    return mlp(jnp.stack(axes).astype(jnp.int32), rows, up_bias[None, :], pieces)


def solution(mesh):
    fine = Mesh(mesh.devices.reshape(8, 4, 2, 4, 2), ("zl", "x", "zh", "y", "c"))
    dp, mp = ("zl", "x"), ("zh", "y", "c")
    return jax.shard_map(
        local,
        mesh=fine,
        in_specs=(P(dp, mp), P(), P(), P(mp), P(dp, mp), P(mp)),
        out_specs=P(dp, mp),
        check_vma=False,
    )
```

time: 233 us -> 228 us (0.979)
  other arithmetic: 23.4 us -> 3.89 us
  starting transfers between devices: 37.1 us -> 45.2 us
  Pallas kernels: 12.8 us -> 17.5 us
  waiting for transfers between devices: 129 us -> 133 us
    add x1, other arithmetic: 15.7 us -> 0.01 us  [local(): flat_index = source * slots + slot_index]
    ppermute x5, waiting for transfers between devices: 64.7 us -> 51.4 us  [shift(): lax.ppermute(value, axis, [(i, (i + step) % size) for i in range(size)])]
    all_gather x2, waiting for transfers between devices: 2.48 us -> 9.99 us  [local(): rows = [lax.all_gather(part, ('y', 'c'), axis=0) for part in (mine, other)]]
    all_to_all x0 -> x1, waiting for transfers between devices: none -> 6.59 us  [local(): lax.all_to_all(copies, 'x', split_axis=0, concat_axis=0, tiled=True)]
    unnamed x16 -> x18, local copies, waits for them, and re-layouts: 6.31 us -> 0.11 us
    all_to_all x0 -> x1, starting transfers between devices: none -> 4.87 us  [local(): lax.all_to_all(copies, 'x', split_axis=0, concat_axis=0, tiled=True)]
    pallas_call x1, Pallas kernels: 12.8 us -> 17.5 us  [mlp(): pl.pallas_call(mlp_kernel, out_shape=jax.ShapeDtypeStruct((RECV, COLS), j...]
    gather x2 -> x0, other arithmetic: 4.51 us -> none  [local(): slot_index = positions - jnp.take(exclusive, source)]
  transfers between devices with their start and end apart: 9 -> 10, of which waited for: 7 -> 8; matrix products, arithmetic and copies ran while one was open for 14% -> 8% of each run, Pallas kernels for 0% -> 0%
where the time goes in v3:
time: 228 us; the launch traced here: 227 us
  waiting for transfers between devices  133 us (58%)
  starting transfers between devices  45.2 us (20%)
  Pallas kernels  17.5 us (8%)
  local copies, waits for them, and re-layouts  14.4 us (6%)
  between operations  13.4 us (6%)
  other arithmetic  3.89 us (2%)
    all_to_all x1, waiting for transfers between devices, local(): lax.all_to_all(outgoing, ('zl', 'x'), split_axis=0, concat_axis=0, tiled=...  63.8 us
    ppermute x5, waiting for transfers between devices, shift(): lax.ppermute(value, axis, [(i, (i + step) % size) for i in range(size)])  51.4 us
    ppermute x5, starting transfers between devices, shift(): lax.ppermute(value, axis, [(i, (i + step) % size) for i in range(size)])  22.2 us
    all_to_all x1, starting transfers between devices, local(): lax.all_to_all(outgoing, ('zl', 'x'), split_axis=0, concat_axis=0, tiled=...  18.1 us
    pallas_call x1, Pallas kernels, mlp(): pl.pallas_call(mlp_kernel, out_shape=jax.ShapeDtypeStruct((RECV, COLS), j...  17.5 us
    all_gather x2, waiting for transfers between devices, local(): rows = [lax.all_gather(part, ('y', 'c'), axis=0) for part in (mine, other)]  9.99 us
    all_to_all x1, waiting for transfers between devices, local(): lax.all_to_all(copies, 'x', split_axis=0, concat_axis=0, tiled=True)  6.59 us
    all_to_all x1, starting transfers between devices, local(): lax.all_to_all(copies, 'x', split_axis=0, concat_axis=0, tiled=True)  4.87 us
  transfers between devices with their start and end apart: 10, of which 8 were waited for; matrix products, arithmetic and copies ran while one was open for 8% of the time, Pallas kernels for 0%

profile of v3, /device:TPU:1, one launch (start us, length us, event | category | flops | bytes accessed | tf_op | source)
XLA Modules:
  0.0 227.0 jit_solution(1403627682470465675)
XLA Ops:
  6.5 0.7 all-gather.6.cloned.1.call-update
  7.3 2.1 broadcast_in_dim.64
  9.3 4.9 %all-to-all-start = ((bf16[4,192,768]{2,1,0:T(8,128)(2,1)}), bf16[4,192,768]{2,1,0:T(8,128)(2,1)S(1)}, u32[]{:S(2)}, u32[]{:S(2)}) async-start(bf16[4,192,768]{2,1,0:T(8,128)(2,1)} %broadcast_in_dim.64), calls=%async_computation | async-start | bytes 2359296 | tf_op jit(solution)/shard_map/all_to_all | solution.py:128
  14.2 0.1 copy.10
  14.3 0.8 sort.17
  15.1 0.2 dynamic-slice_reduce_fusion
  15.3 0.0 copy-done.1
  15.3 0.7 gather_fusion.2
  16.1 0.1 copy.11
  16.1 0.1 reduce-window.7
  16.2 0.1 reduce.2
  16.3 0.1 convert_reduce_fusion
  16.4 0.1 select_reduce_fusion
  16.5 0.0 copy-done
  16.5 0.7 gather_fusion
  17.3 1.0 broadcast_select_fusion
  18.3 6.6 %all-to-all-done = bf16[4,192,768]{2,1,0:T(8,128)(2,1)S(1)} async-done(((bf16[4,192,768]{2,1,0:T(8,128)(2,1)}), bf16[4,192,768]{2,1,0:T(8,128)(2,1)S(1)}, u32[]{:S(2)}, u32[]{:S(2)}) %all-to-all-start) | async-done | bytes 1179680 | tf_op jit(solution)/shard_map/all_to_all | solution.py:128
  24.9 18.1 %all-to-all-start.1 = ((bf16[32,32,384]{2,1,0:T(8,128)(2,1)}), bf16[32,32,384]{2,1,0:T(8,128)(2,1)S(1)}, u32[]{:S(2)}, u32[]{:S(2)}) async-start(bf16[32,32,384]{2,1,0:T(8,128)(2,1)} %broadcast_select_fusion), calls=%async_computation.1 | async-start | bytes 1572864 | tf_op jit(solution)/shard_map/all_to_all | solution.py:151
  43.0 0.0 all-gather.8.cloned.1.call-start
  43.1 63.8 %all-to-all-done.1 = bf16[32,32,384]{2,1,0:T(8,128)(2,1)S(1)} async-done(((bf16[32,32,384]{2,1,0:T(8,128)(2,1)}), bf16[32,32,384]{2,1,0:T(8,128)(2,1)S(1)}, u32[]{:S(2)}, u32[]{:S(2)}) %all-to-all-start.1) | async-done | bytes 786464 | tf_op jit(solution)/shard_map/all_to_all | solution.py:151
  106.9 0.0 copy-done.4
  106.9 1.9 gather_fusion.1
  108.9 0.1 broadcast_select_fusion.1
  109.0 0.8 pad_maximum_fusion
  109.8 0.0 all-gather.8.cloned.1.call-update
  109.8 0.0 all-gather.10.cloned.1.call-start
  109.9 0.0 all-gather.6.cloned.1.call-done
  109.9 1.0 slice.22
  110.9 0.7 constant_dynamic-update-slice_fusion
  111.7 1.8 slice.23.refs_1_
  113.4 3.4 %collective-permute-start.1 = (bf16[1344,768]{1,0:T(8,128)(2,1)S(1)}, bf16[1344,768]{1,0:T(8,128)(2,1)}, u32[]{:S(2)}, u32[]{:S(2)}) collective-permute-start(bf16[1344,768]{1,0:T(8,128)(2,1)S(1)} %slice.23.refs_1_), channel_id=1, source_target_pairs={{0,16},{16,32},{32,48},{48,0},{1,17},{17,33},{33,49},{49,1},{2,18}... | collective-permute-start | bytes 6193160 | tf_op jit(solution)/shard_map/ppermute | solution.py:23
  116.8 3.7 %collective-permute-start.2 = (bf16[1344,768]{1,0:T(8,128)(2,1)S(1)}, bf16[1344,768]{1,0:T(8,128)(2,1)}, u32[]{:S(2)}, u32[]{:S(2)}) collective-permute-start(bf16[1344,768]{1,0:T(8,128)(2,1)S(1)} %slice.23.refs_1_), channel_id=1, source_target_pairs={{0,48},{16,0},{32,16},{48,32},{1,49},{17,1},{33,17},{49,33},{2,50}... | collective-permute-start | bytes 6193160 | tf_op jit(solution)/shard_map/ppermute | solution.py:23
  120.6 8.3 %collective-permute-start = (bf16[528,384]{1,0:T(8,128)(2,1)S(1)}, bf16[528,384]{1,0:T(8,128)(2,1)}, u32[]{:S(2)}, u32[]{:S(2)}) collective-permute-start(bf16[528,384]{1,0:T(8,128)(2,1)S(1)} %copy-done.3), channel_id=1, source_target_pairs={{0,8},{8,0},{1,9},{9,1},{2,10},{10,2},{3,11},{11,3},{4,12},{12,4},... | collective-permute-start | bytes 1216520 | tf_op jit(solution)/shard_map/ppermute | solution.py:23
  128.9 11.3 %collective-permute-done = bf16[528,384]{1,0:T(8,128)(2,1)} collective-permute-done((bf16[528,384]{1,0:T(8,128)(2,1)S(1)}, bf16[528,384]{1,0:T(8,128)(2,1)}, u32[]{:S(2)}, u32[]{:S(2)}) %collective-permute-start) | collective-permute-done | bytes 405536 | tf_op jit(solution)/shard_map/ppermute | solution.py:23
  140.2 21.2 %collective-permute-done.1.refs_2_ = bf16[1344,768]{1,0:T(8,128)(2,1)} collective-permute-done((bf16[1344,768]{1,0:T(8,128)(2,1)S(1)}, bf16[1344,768]{1,0:T(8,128)(2,1)}, u32[]{:S(2)}, u32[]{:S(2)}) %collective-permute-start.1) | collective-permute-done | bytes 2064416 | tf_op jit(solution)/shard_map/ppermute | solution.py:23
  161.3 1.4 collective-permute-done.2.refs_3_
  162.7 0.0 all-gather.10.cloned.1.call-update
  162.7 0.0 copy-start.6
  162.8 2.4 %slice.24 = bf16[768,768]{1,0:T(8,128)(2,1)} slice(bf16[1344,768]{1,0:T(8,128)(2,1)} %collective-permute-done.1.refs_2_), slice={[0:768], [0:768]} | slice | bytes 2359296 | tf_op jit(solution)/shard_map/slice | solution.py:118
  165.1 3.6 %collective-permute-start.3 = (bf16[768,768]{1,0:T(8,128)(2,1)}, bf16[768,768]{1,0:T(8,128)(2,1)}, u32[]{:S(2)}, u32[]{:S(2)}) collective-permute-start(bf16[768,768]{1,0:T(8,128)(2,1)} %slice.24), channel_id=1, source_target_pairs={{0,16},{16,32},{32,48},{48,0},{1,17},{17,33},{33,49},{49,1},{2,18}... | collective-permute-start | bytes 3538952 | tf_op jit(solution)/shard_map/ppermute | solution.py:23
  168.8 2.2 slice.25
  170.9 3.1 %collective-permute-start.4 = (bf16[576,768]{1,0:T(8,128)(2,1)}, bf16[576,768]{1,0:T(8,128)(2,1)}, u32[]{:S(2)}, u32[]{:S(2)}) collective-permute-start(bf16[576,768]{1,0:T(8,128)(2,1)} %slice.25), channel_id=1, source_target_pairs={{0,48},{16,0},{32,16},{48,32},{1,49},{17,1},{33,17},{49,33},{2,50}... | collective-permute-start | bytes 2654216 | tf_op jit(solution)/shard_map/ppermute | solution.py:23
  174.1 0.6 broadcast_in_dim.69.bias_ref
  174.7 0.7 pad_add_fusion.place_ref
  175.3 15.3 %collective-permute-done.4.refs_5_ = bf16[576,768]{1,0:T(8,128)(2,1)} collective-permute-done((bf16[576,768]{1,0:T(8,128)(2,1)}, bf16[576,768]{1,0:T(8,128)(2,1)}, u32[]{:S(2)}, u32[]{:S(2)}) %collective-permute-start.4) | collective-permute-done | bytes 884768 | tf_op jit(solution)/shard_map/ppermute | solution.py:23
  190.6 2.3 %collective-permute-done.3.refs_4_ = bf16[768,768]{1,0:T(8,128)(2,1)} collective-permute-done((bf16[768,768]{1,0:T(8,128)(2,1)}, bf16[768,768]{1,0:T(8,128)(2,1)}, u32[]{:S(2)}, u32[]{:S(2)}) %collective-permute-start.3) | collective-permute-done | bytes 1179680 | tf_op jit(solution)/shard_map/ppermute | solution.py:23
  192.9 10.0 %all-gather.10.cloned.1.call-done = bf16[4224,384]{1,0:T(8,128)(2,1)} async-done(((bf16[528,384]{1,0:T(8,128)(2,1)}), bf16[4224,384]{1,0:T(8,128)(2,1)}) %all-gather.10.cloned.1.call-update) | async-done | bytes 3244048 | tf_op jit(solution)/shard_map/all_gather | solution.py:159
  202.9 17.5 %shard_map.64 = bf16[512,768]{1,0:T(8,128)(2,1)} custom-call(s32[3]{0:T(128)} %pad_add_fusion.place_ref, bf16[8,528,384]{2,1,0:T(8,128)(2,1)} %bitcast.25, bf16[8,528,384]{2,1,0:T(8,128)(2,1)} %bitcast.26, bf16[1,768]{1,0:T(2,128)(2,1)} %broadcast_in_dim.69.bias_ref, bf16[768,768]{1,0:T(8,128)(2,1)} %bitcast.24, bf16[1344,768]{1,0:T(8,128)(2,1)} %copy-done.2, ...), custom_call_target="tpu_custom_call" | custom-call | flops 4831838208 | bytes 15728640 | tf_op jit(solution)/shard_map/pallas_call | solution.py:93
  (28 shorter events, 0.1 us)
Async XLA Ops:
  6.5 10.0 %copy-start = (bf16[1024,384]{1,0:T(8,128)(2,1)S(1)}, bf16[1024,384]{1,0:T(8,128)(2,1)}, u32[]{:S(2)}) copy-start(bf16[1024,384]{1,0:T(8,128)(2,1)} %param.6) | copy-start | bytes 2359300
  6.5 7.7 %copy-start.5 = (s32[32,32]{1,0:T(8,128)S(1)}, s32[32,32]{1,0:T(8,128)}, u32[]{:S(2)}) copy-start(s32[32,32]{1,0:T(8,128)} %param.8) | copy-start | bytes 12292
  6.5 8.8 %copy-start.1 = (s32[32,32]{1,0:T(8,128)S(1)}, s32[32,32]{1,0:T(8,128)}, u32[]{:S(2)}) copy-start(s32[32,32]{1,0:T(8,128)} %param.7) | copy-start | bytes 12292
  6.5 103.4 %all-gather.6.cloned.1.call-start = ((), (), s32[]{:S(2)}) async-start(), calls=%async_computation.2 | async-start | bytes 2654208 | tf_op jit(solution)/shard_map/all_gather | solution.py:129
  9.3 15.6 %all-to-all-start = ((bf16[4,192,768]{2,1,0:T(8,128)(2,1)}), bf16[4,192,768]{2,1,0:T(8,128)(2,1)S(1)}, u32[]{:S(2)}, u32[]{:S(2)}) async-start(bf16[4,192,768]{2,1,0:T(8,128)(2,1)} %broadcast_in_dim.64), calls=%async_computation | async-start | bytes 2359296 | tf_op jit(solution)/shard_map/all_to_all | solution.py:128
  24.9 82.0 %copy-start.4 = (bf16[4,192,768]{2,1,0:T(8,128)(2,1)}, bf16[4,192,768]{2,1,0:T(8,128)(2,1)S(1)}, u32[]{:S(2)}) copy-start(bf16[4,192,768]{2,1,0:T(8,128)(2,1)S(1)} %all-to-all-done) | copy-start | bytes 3538948
  24.9 82.0 %all-to-all-start.1 = ((bf16[32,32,384]{2,1,0:T(8,128)(2,1)}), bf16[32,32,384]{2,1,0:T(8,128)(2,1)S(1)}, u32[]{:S(2)}, u32[]{:S(2)}) async-start(bf16[32,32,384]{2,1,0:T(8,128)(2,1)} %broadcast_select_fusion), calls=%async_computation.1 | async-start | bytes 1572864 | tf_op jit(solution)/shard_map/all_to_all | solution.py:151
  43.0 149.9 %all-gather.8.cloned.1.call-start = ((), (), s32[]{:S(2)}) async-start(), calls=%async_computation.3 | async-start | bytes 3649536 | tf_op jit(solution)/shard_map/all_gather | solution.py:159
  106.9 2.1 copy-start.7
  109.8 93.1 %all-gather.10.cloned.1.call-start = ((), (), s32[]{:S(2)}) async-start(), calls=%async_computation.4 | async-start | bytes 3649536 | tf_op jit(solution)/shard_map/all_gather | solution.py:159
  111.7 8.9 %copy-start.3 = (bf16[528,384]{1,0:T(8,128)(2,1)S(1)}, bf16[528,384]{1,0:T(8,128)(2,1)}, u32[]{:S(2)}) copy-start(bf16[528,384]{1,0:T(8,128)(2,1)} %pad_maximum_fusion) | copy-start | bytes 1216516
  113.4 57.5 %copy-start.2 = (bf16[1344,768]{1,0:T(8,128)(2,1)}, bf16[1344,768]{1,0:T(8,128)(2,1)S(1)}, u32[]{:S(2)}) copy-start(bf16[1344,768]{1,0:T(8,128)(2,1)S(1)} %slice.23.refs_1_) | copy-start | bytes 6193156
  113.4 47.9 %collective-permute-start.1 = (bf16[1344,768]{1,0:T(8,128)(2,1)S(1)}, bf16[1344,768]{1,0:T(8,128)(2,1)}, u32[]{:S(2)}, u32[]{:S(2)}) collective-permute-start(bf16[1344,768]{1,0:T(8,128)(2,1)S(1)} %slice.23.refs_1_), channel_id=1, source_target_pairs={{0,16},{16,32},{32,48},{48,0},{1,17},{17,33},{33,49},{49,1},{2,18}... | collective-permute-start | bytes 6193160 | tf_op jit(solution)/shard_map/ppermute | solution.py:23
  116.8 45.9 %collective-permute-start.2 = (bf16[1344,768]{1,0:T(8,128)(2,1)S(1)}, bf16[1344,768]{1,0:T(8,128)(2,1)}, u32[]{:S(2)}, u32[]{:S(2)}) collective-permute-start(bf16[1344,768]{1,0:T(8,128)(2,1)S(1)} %slice.23.refs_1_), channel_id=1, source_target_pairs={{0,48},{16,0},{32,16},{48,32},{1,49},{17,1},{33,17},{49,33},{2,50}... | collective-permute-start | bytes 6193160 | tf_op jit(solution)/shard_map/ppermute | solution.py:23
  120.6 19.6 %collective-permute-start = (bf16[528,384]{1,0:T(8,128)(2,1)S(1)}, bf16[528,384]{1,0:T(8,128)(2,1)}, u32[]{:S(2)}, u32[]{:S(2)}) collective-permute-start(bf16[528,384]{1,0:T(8,128)(2,1)S(1)} %copy-done.3), channel_id=1, source_target_pairs={{0,8},{8,0},{1,9},{9,1},{2,10},{10,2},{3,11},{11,3},{4,12},{12,4},... | collective-permute-start | bytes 1216520 | tf_op jit(solution)/shard_map/ppermute | solution.py:23
  162.7 11.3 %copy-start.6 = (bf16[768]{0:T(1024)(128)(2,1)S(1)}, bf16[768]{0:T(1024)(128)(2,1)}, u32[]{:S(2)}) copy-start(bf16[768]{0:T(1024)(128)(2,1)} %param.11) | copy-start | bytes 4612
  165.1 27.8 %collective-permute-start.3 = (bf16[768,768]{1,0:T(8,128)(2,1)}, bf16[768,768]{1,0:T(8,128)(2,1)}, u32[]{:S(2)}, u32[]{:S(2)}) collective-permute-start(bf16[768,768]{1,0:T(8,128)(2,1)} %slice.24), channel_id=1, source_target_pairs={{0,16},{16,32},{32,48},{48,0},{1,17},{17,33},{33,49},{49,1},{2,18}... | collective-permute-start | bytes 3538952 | tf_op jit(solution)/shard_map/ppermute | solution.py:23
  170.9 19.7 %collective-permute-start.4 = (bf16[576,768]{1,0:T(8,128)(2,1)}, bf16[576,768]{1,0:T(8,128)(2,1)}, u32[]{:S(2)}, u32[]{:S(2)}) collective-permute-start(bf16[576,768]{1,0:T(8,128)(2,1)} %slice.25), channel_id=1, source_target_pairs={{0,48},{16,0},{32,16},{48,32},{1,49},{17,1},{33,17},{49,33},{2,50}... | collective-permute-start | bytes 2654216 | tf_op jit(solution)/shard_map/ppermute | solution.py:23
Sparse Core Ops, SparseCore 0:
  9.4 97.1 all-gather.5
  110.0 40.7 all-gather.7
  162.9 40.0 all-gather.9

commit v4 on v3

--- a/solution.py
+++ b/solution.py
@@ -15,6 +15,8 @@
 GAIN_ROWS = 16
 ROWS = RECV + GAIN_ROWS
 STRIP = 32
+CHUNK = 128
+NEAR_MIB = 58
 VMEM_MIB = 60
 INV_SQRT2 = 0.7071067811865476
 
@@ -45,38 +47,58 @@
     return copies
 
 
-def mlp_kernel(place_ref, near_ref, far_ref, bias_ref, *refs):
+def row_sums(rows_ref, first, rows, total, square):
+    for index in range(first, first + 8):
+        for lane in range(PART // 128):
+            v = rows_ref[index, rows, lane * 128 : (lane + 1) * 128].astype(jnp.float32)
+            total += v
+            square += v * v
+    return total, square
+
+
+def near_kernel(near_ref, sums_ref, rows_ref, sem):
+    inward = pltpu.make_async_copy(near_ref, rows_ref, sem)
+    inward.start()
+    inward.wait()
+
+    @pl.loop(0, RECV // STRIP)
+    def _(strip):
+        rows = pl.ds(pl.multiple_of(strip * STRIP, STRIP), STRIP)
+        zero = jnp.zeros((STRIP, 128), jnp.float32)
+        sums_ref[0, rows, :], sums_ref[1, rows, :] = row_sums(rows_ref, 0, rows, zero, zero)
+
+
+def mlp_kernel(place_ref, sums_ref, near_ref, far_ref, bias_ref, *refs):
     pieces, (out_ref, rows_ref, w_ref, normed_ref, row_sems, sems) = refs[:6], refs[6:]
     half = place_ref[1]
+    blocks = [pl.ds(RECV, GAIN_ROWS)] + [pl.ds(i * CHUNK, CHUNK) for i in range(RECV // CHUNK)]
     inward = [
-        pltpu.make_async_copy(ref, rows_ref.at[pl.ds(8 * side, 8)], row_sems.at[side])
+        pltpu.make_async_copy(ref.at[:, block, :], rows_ref.at[pl.ds(8 * side, 8), block, :], row_sems.at[2 * i + side])
+        for i, block in enumerate(blocks)
         for side, ref in enumerate((near_ref, far_ref))
     ]
     copies = row_copies(place_ref, pieces, w_ref, sems)
     for copy in inward + copies:
         copy.start()
-    for copy in inward:
-        copy.wait()
-
-    @pl.loop(0, RECV // STRIP)
-    def _(strip):
-        rows = pl.ds(pl.multiple_of(strip * STRIP, STRIP), STRIP)
-        total = jnp.zeros((STRIP, 128), jnp.float32)
-        square = jnp.zeros((STRIP, 128), jnp.float32)
-        for index in range(16):
-            for lane in range(PART // 128):
-                v = rows_ref[index, rows, lane * 128 : (lane + 1) * 128].astype(jnp.float32)
-                total += v
-                square += v * v
-        row_mean = jnp.sum(total, axis=1, keepdims=True) / D
-        variance = jnp.sum(square, axis=1, keepdims=True) / D - row_mean * row_mean
-        scale = lax.rsqrt(variance + 1e-06)
-        for index in range(16):
-            v = rows_ref[index, rows, :].astype(jnp.float32)
-            gain = rows_ref[index, RECV : RECV + 1, :].astype(jnp.float32)
-            at = 8 * lax.rem(half + index // 8, 2) + index % 8
-            columns = pl.ds(pl.multiple_of(at * PART, 128), PART)
-            normed_ref[rows, columns] = ((v - row_mean) * scale * gain).astype(jnp.bfloat16)
+    inward[0].wait()
+    inward[1].wait()
+    for chunk in range(RECV // CHUNK):
+        inward[2 + 2 * chunk].wait()
+        inward[3 + 2 * chunk].wait()
+
+        @pl.loop(chunk * (CHUNK // STRIP), (chunk + 1) * (CHUNK // STRIP))
+        def _(strip):
+            rows = pl.ds(pl.multiple_of(strip * STRIP, STRIP), STRIP)
+            total, square = row_sums(rows_ref, 8, rows, sums_ref[0, rows, :], sums_ref[1, rows, :])
+            row_mean = jnp.sum(total, axis=1, keepdims=True) / D
+            variance = jnp.sum(square, axis=1, keepdims=True) / D - row_mean * row_mean
+            scale = lax.rsqrt(variance + 1e-06)
+            for index in range(16):
+                v = rows_ref[index, rows, :].astype(jnp.float32)
+                gain = rows_ref[index, RECV : RECV + 1, :].astype(jnp.float32)
+                at = 8 * lax.rem(half + index // 8, 2) + index % 8
+                columns = pl.ds(pl.multiple_of(at * PART, 128), PART)
+                normed_ref[rows, columns] = ((v - row_mean) * scale * gain).astype(jnp.bfloat16)
 
     for copy in copies:
         copy.wait()
@@ -88,25 +110,35 @@
 
 
 def mlp(place, rows, bias, pieces):
+    near, far = rows
     vmem = pl.BlockSpec(memory_space=pltpu.VMEM)
     left = pl.BlockSpec(memory_space=pl.ANY)
+    sums = pl.pallas_call(
+        near_kernel,
+        out_shape=jax.ShapeDtypeStruct((2, RECV, 128), jnp.float32),
+        in_specs=[left],
+        out_specs=vmem,
+        scratch_shapes=[pltpu.VMEM((8, ROWS, PART), jnp.bfloat16), pltpu.SemaphoreType.DMA],
+        compiler_params=pltpu.CompilerParams(vmem_limit_bytes=NEAR_MIB * 1024 * 1024),
+        cost_estimate=pl.CostEstimate(flops=2 * RECV * D, bytes_accessed=2 * RECV * D, transcendentals=0),
+    )(near)
     return pl.pallas_call(
         mlp_kernel,
         out_shape=jax.ShapeDtypeStruct((RECV, COLS), jnp.bfloat16),
-        in_specs=[pl.BlockSpec(memory_space=pltpu.SMEM)] + [left] * 2 + [vmem] + [left] * 6,
+        in_specs=[pl.BlockSpec(memory_space=pltpu.SMEM), vmem, left, left, vmem] + [left] * 6,
         out_specs=vmem,
         scratch_shapes=[
             pltpu.VMEM((16, ROWS, PART), jnp.bfloat16),
             pltpu.VMEM((D, COLS), jnp.bfloat16),
             pltpu.VMEM((RECV, D), jnp.bfloat16),
-            pltpu.SemaphoreType.DMA((2,)),
+            pltpu.SemaphoreType.DMA((10,)),
             pltpu.SemaphoreType.DMA((29,)),
         ],
         compiler_params=pltpu.CompilerParams(vmem_limit_bytes=VMEM_MIB * 1024 * 1024),
         cost_estimate=pl.CostEstimate(
             flops=2 * RECV * D * COLS, bytes_accessed=2 * (RECV * D + D * COLS), transcendentals=RECV * COLS
         ),
-    )(place, *rows, bias, *pieces)
+    )(place, sums, near, far, bias, *pieces)
 
 
 def beside(own):

time: 228 us -> 225 us (0.987)
  waiting for transfers between devices: 133 us -> 129 us
    pallas_call x0 -> x1, Pallas kernels: none -> 3.8 us  [mlp(): pl.pallas_call(near_kernel, out_shape=jax.ShapeDtypeStruct((2, RECV, 128)...]
    ppermute x5, waiting for transfers between devices: 51.4 us -> 47.7 us  [shift(): lax.ppermute(value, axis, [(i, (i + step) % size) for i in range(size)])]
    pallas_call x1, Pallas kernels: 17.5 us -> 15 us  [mlp(): pl.pallas_call(mlp_kernel, out_shape=jax.ShapeDtypeStruct((RECV, COLS), j...]
  transfers between devices with their start and end apart: 10 -> 10, of which waited for: 8 -> 8; matrix products, arithmetic and copies ran while one was open for 8% -> 8% of each run, Pallas kernels for 0% -> 2%
where the time goes in v4:
time: 225 us; the launch traced here: 224 us
  waiting for transfers between devices  129 us (57%)
  starting transfers between devices  45.2 us (20%)
  Pallas kernels  18.8 us (8%)
  local copies, waits for them, and re-layouts  14.4 us (6%)
  between operations  13.4 us (6%)
  other arithmetic  3.83 us (2%)
    all_to_all x1, waiting for transfers between devices, local(): lax.all_to_all(outgoing, ('zl', 'x'), split_axis=0, concat_axis=0, tiled=...  63.8 us
    ppermute x5, waiting for transfers between devices, shift(): lax.ppermute(value, axis, [(i, (i + step) % size) for i in range(size)])  47.7 us
    ppermute x5, starting transfers between devices, shift(): lax.ppermute(value, axis, [(i, (i + step) % size) for i in range(size)])  22.2 us
    all_to_all x1, starting transfers between devices, local(): lax.all_to_all(outgoing, ('zl', 'x'), split_axis=0, concat_axis=0, tiled=...  18.1 us
    pallas_call x1, Pallas kernels, mlp(): pl.pallas_call(mlp_kernel, out_shape=jax.ShapeDtypeStruct((RECV, COLS), j...  15 us
    all_gather x2, waiting for transfers between devices, local(): rows = [lax.all_gather(part, ('y', 'c'), axis=0) for part in (mine, other)]  10 us
    all_to_all x1, waiting for transfers between devices, local(): lax.all_to_all(copies, 'x', split_axis=0, concat_axis=0, tiled=True)  6.59 us
    all_to_all x1, starting transfers between devices, local(): lax.all_to_all(copies, 'x', split_axis=0, concat_axis=0, tiled=True)  4.87 us
  transfers between devices with their start and end apart: 10, of which 8 were waited for; matrix products, arithmetic and copies ran while one was open for 8% of the time, Pallas kernels for 2%

profile of v4, /device:TPU:1, one launch (start us, length us, event | category | flops | bytes accessed | tf_op | source)
XLA Modules:
  0.0 224.4 jit_solution(11995893146235533442)
XLA Ops:
  6.5 0.7 all-gather.6.cloned.1.call-update
  7.3 2.1 broadcast_in_dim.64
  9.3 4.9 %all-to-all-start = ((bf16[4,192,768]{2,1,0:T(8,128)(2,1)}), bf16[4,192,768]{2,1,0:T(8,128)(2,1)S(1)}, u32[]{:S(2)}, u32[]{:S(2)}) async-start(bf16[4,192,768]{2,1,0:T(8,128)(2,1)} %broadcast_in_dim.64), calls=%async_computation | async-start | bytes 2359296 | tf_op jit(solution)/shard_map/all_to_all | solution.py:160
  14.2 0.1 copy.10
  14.3 0.8 sort.17
  15.1 0.2 dynamic-slice_reduce_fusion
  15.3 0.7 gather_fusion.2
  16.1 0.1 copy.11
  16.1 0.1 reduce-window.7
  16.2 0.1 reduce.2
  16.3 0.1 convert_reduce_fusion
  16.4 0.1 select_reduce_fusion
  16.5 0.7 gather_fusion
  17.3 1.0 broadcast_select_fusion
  18.3 6.6 %all-to-all-done = bf16[4,192,768]{2,1,0:T(8,128)(2,1)S(1)} async-done(((bf16[4,192,768]{2,1,0:T(8,128)(2,1)}), bf16[4,192,768]{2,1,0:T(8,128)(2,1)S(1)}, u32[]{:S(2)}, u32[]{:S(2)}) %all-to-all-start) | async-done | bytes 1179680 | tf_op jit(solution)/shard_map/all_to_all | solution.py:160
  24.9 18.1 %all-to-all-start.1 = ((bf16[32,32,384]{2,1,0:T(8,128)(2,1)}), bf16[32,32,384]{2,1,0:T(8,128)(2,1)S(1)}, u32[]{:S(2)}, u32[]{:S(2)}) async-start(bf16[32,32,384]{2,1,0:T(8,128)(2,1)} %broadcast_select_fusion), calls=%async_computation.1 | async-start | bytes 1572864 | tf_op jit(solution)/shard_map/all_to_all | solution.py:183
  43.0 0.0 all-gather.8.cloned.1.call-start
  43.1 63.8 %all-to-all-done.1 = bf16[32,32,384]{2,1,0:T(8,128)(2,1)S(1)} async-done(((bf16[32,32,384]{2,1,0:T(8,128)(2,1)}), bf16[32,32,384]{2,1,0:T(8,128)(2,1)S(1)}, u32[]{:S(2)}, u32[]{:S(2)}) %all-to-all-start.1) | async-done | bytes 786464 | tf_op jit(solution)/shard_map/all_to_all | solution.py:183
  106.9 1.9 gather_fusion.1
  108.9 0.1 broadcast_select_fusion.1
  109.0 0.8 pad_maximum_fusion
  109.8 0.0 all-gather.8.cloned.1.call-update
  109.8 0.0 all-gather.10.cloned.1.call-start
  109.9 0.0 all-gather.6.cloned.1.call-done
  109.9 1.0 slice.22
  110.9 0.7 constant_dynamic-update-slice_fusion
  111.7 1.8 slice.23.refs_1_
  113.4 3.4 %collective-permute-start.1 = (bf16[1344,768]{1,0:T(8,128)(2,1)S(1)}, bf16[1344,768]{1,0:T(8,128)(2,1)}, u32[]{:S(2)}, u32[]{:S(2)}) collective-permute-start(bf16[1344,768]{1,0:T(8,128)(2,1)S(1)} %slice.23.refs_1_), channel_id=1, source_target_pairs={{0,16},{16,32},{32,48},{48,0},{1,17},{17,33},{33,49},{49,1},{2,18}... | collective-permute-start | bytes 6193160 | tf_op jit(solution)/shard_map/ppermute | solution.py:25
  116.8 3.7 %collective-permute-start.2 = (bf16[1344,768]{1,0:T(8,128)(2,1)S(1)}, bf16[1344,768]{1,0:T(8,128)(2,1)}, u32[]{:S(2)}, u32[]{:S(2)}) collective-permute-start(bf16[1344,768]{1,0:T(8,128)(2,1)S(1)} %slice.23.refs_1_), channel_id=1, source_target_pairs={{0,48},{16,0},{32,16},{48,32},{1,49},{17,1},{33,17},{49,33},{2,50}... | collective-permute-start | bytes 6193160 | tf_op jit(solution)/shard_map/ppermute | solution.py:25
  120.6 0.0 copy-done.3
  120.6 8.3 %collective-permute-start = (bf16[528,384]{1,0:T(8,128)(2,1)S(1)}, bf16[528,384]{1,0:T(8,128)(2,1)}, u32[]{:S(2)}, u32[]{:S(2)}) collective-permute-start(bf16[528,384]{1,0:T(8,128)(2,1)S(1)} %copy-done.3), channel_id=1, source_target_pairs={{0,8},{8,0},{1,9},{9,1},{2,10},{10,2},{3,11},{11,3},{4,12},{12,4},... | collective-permute-start | bytes 1216520 | tf_op jit(solution)/shard_map/ppermute | solution.py:25
  128.9 11.3 %collective-permute-done = bf16[528,384]{1,0:T(8,128)(2,1)} collective-permute-done((bf16[528,384]{1,0:T(8,128)(2,1)S(1)}, bf16[528,384]{1,0:T(8,128)(2,1)}, u32[]{:S(2)}, u32[]{:S(2)}) %collective-permute-start) | collective-permute-done | bytes 405536 | tf_op jit(solution)/shard_map/ppermute | solution.py:25
  140.2 21.2 %collective-permute-done.1.refs_2_ = bf16[1344,768]{1,0:T(8,128)(2,1)} collective-permute-done((bf16[1344,768]{1,0:T(8,128)(2,1)S(1)}, bf16[1344,768]{1,0:T(8,128)(2,1)}, u32[]{:S(2)}, u32[]{:S(2)}) %collective-permute-start.1) | collective-permute-done | bytes 2064416 | tf_op jit(solution)/shard_map/ppermute | solution.py:25
  161.3 1.4 collective-permute-done.2.refs_3_
  162.7 0.0 all-gather.10.cloned.1.call-update
  162.7 0.0 copy-start.6
  162.8 2.4 %slice.24 = bf16[768,768]{1,0:T(8,128)(2,1)} slice(bf16[1344,768]{1,0:T(8,128)(2,1)} %collective-permute-done.1.refs_2_), slice={[0:768], [0:768]} | slice | bytes 2359296 | tf_op jit(solution)/shard_map/slice | solution.py:150
  165.1 3.6 %collective-permute-start.3 = (bf16[768,768]{1,0:T(8,128)(2,1)}, bf16[768,768]{1,0:T(8,128)(2,1)}, u32[]{:S(2)}, u32[]{:S(2)}) collective-permute-start(bf16[768,768]{1,0:T(8,128)(2,1)} %slice.24), channel_id=1, source_target_pairs={{0,16},{16,32},{32,48},{48,0},{1,17},{17,33},{33,49},{49,1},{2,18}... | collective-permute-start | bytes 3538952 | tf_op jit(solution)/shard_map/ppermute | solution.py:25
  168.8 2.2 slice.25
  170.9 3.1 %collective-permute-start.4 = (bf16[576,768]{1,0:T(8,128)(2,1)}, bf16[576,768]{1,0:T(8,128)(2,1)}, u32[]{:S(2)}, u32[]{:S(2)}) collective-permute-start(bf16[576,768]{1,0:T(8,128)(2,1)} %slice.25), channel_id=1, source_target_pairs={{0,48},{16,0},{32,16},{48,32},{1,49},{17,1},{33,17},{49,33},{2,50}... | collective-permute-start | bytes 2654216 | tf_op jit(solution)/shard_map/ppermute | solution.py:25
  174.1 0.0 copy-done.6
  174.1 0.6 broadcast_in_dim.69.bias_ref
  174.7 0.6 pad_add_fusion.place_ref
  175.3 3.8 %shard_map.64.sums_ref = f32[2,512,128]{2,1,0:T(8,128)} custom-call(bf16[8,528,384]{2,1,0:T(8,128)(2,1)} %bitcast.24), custom_call_target="tpu_custom_call" | custom-call | flops 6291456 | bytes 6291456 | tf_op jit(solution)/shard_map/pallas_call | solution.py:116
  179.1 11.5 %collective-permute-done.4.refs_5_ = bf16[576,768]{1,0:T(8,128)(2,1)} collective-permute-done((bf16[576,768]{1,0:T(8,128)(2,1)}, bf16[576,768]{1,0:T(8,128)(2,1)}, u32[]{:S(2)}, u32[]{:S(2)}) %collective-permute-start.4) | collective-permute-done | bytes 884768 | tf_op jit(solution)/shard_map/ppermute | solution.py:25
  190.6 2.3 %collective-permute-done.3.refs_4_ = bf16[768,768]{1,0:T(8,128)(2,1)} collective-permute-done((bf16[768,768]{1,0:T(8,128)(2,1)}, bf16[768,768]{1,0:T(8,128)(2,1)}, u32[]{:S(2)}, u32[]{:S(2)}) %collective-permute-start.3) | collective-permute-done | bytes 1179680 | tf_op jit(solution)/shard_map/ppermute | solution.py:25
  192.9 10.0 %all-gather.10.cloned.1.call-done = bf16[4224,384]{1,0:T(8,128)(2,1)} async-done(((bf16[528,384]{1,0:T(8,128)(2,1)}), bf16[4224,384]{1,0:T(8,128)(2,1)}) %all-gather.10.cloned.1.call-update) | async-done | bytes 3244048 | tf_op jit(solution)/shard_map/all_gather | solution.py:191
  202.9 15.0 %shard_map.65 = bf16[512,768]{1,0:T(8,128)(2,1)} custom-call(s32[3]{0:T(128)} %pad_add_fusion.place_ref, f32[2,512,128]{2,1,0:T(8,128)} %shard_map.64.sums_ref, bf16[8,528,384]{2,1,0:T(8,128)(2,1)} %bitcast.25, bf16[8,528,384]{2,1,0:T(8,128)(2,1)} %bitcast.27, bf16[1,768]{1,0:T(2,128)(2,1)} %broadcast_in_dim.69.bias_ref, bf16[768,768]{1,0:T(8,128)(2,1)} %bitcast.26, ...), custom_call_target="tpu_custom_call" | custom-call | flops 4831838208 | bytes 15728640 | tf_op jit(solution)/shard_map/pallas_call | solution.py:125
  (29 shorter events, 0.1 us)
Async XLA Ops:
  6.5 10.0 %copy-start = (bf16[1024,384]{1,0:T(8,128)(2,1)S(1)}, bf16[1024,384]{1,0:T(8,128)(2,1)}, u32[]{:S(2)}) copy-start(bf16[1024,384]{1,0:T(8,128)(2,1)} %param.6) | copy-start | bytes 2359300
  6.5 7.7 %copy-start.5 = (s32[32,32]{1,0:T(8,128)S(1)}, s32[32,32]{1,0:T(8,128)}, u32[]{:S(2)}) copy-start(s32[32,32]{1,0:T(8,128)} %param.8) | copy-start | bytes 12292
  6.5 8.8 %copy-start.1 = (s32[32,32]{1,0:T(8,128)S(1)}, s32[32,32]{1,0:T(8,128)}, u32[]{:S(2)}) copy-start(s32[32,32]{1,0:T(8,128)} %param.7) | copy-start | bytes 12292
  6.5 103.4 %all-gather.6.cloned.1.call-start = ((), (), s32[]{:S(2)}) async-start(), calls=%async_computation.2 | async-start | bytes 2654208 | tf_op jit(solution)/shard_map/all_gather | solution.py:161
  9.3 15.6 %all-to-all-start = ((bf16[4,192,768]{2,1,0:T(8,128)(2,1)}), bf16[4,192,768]{2,1,0:T(8,128)(2,1)S(1)}, u32[]{:S(2)}, u32[]{:S(2)}) async-start(bf16[4,192,768]{2,1,0:T(8,128)(2,1)} %broadcast_in_dim.64), calls=%async_computation | async-start | bytes 2359296 | tf_op jit(solution)/shard_map/all_to_all | solution.py:160
  24.9 82.0 %copy-start.4 = (bf16[4,192,768]{2,1,0:T(8,128)(2,1)}, bf16[4,192,768]{2,1,0:T(8,128)(2,1)S(1)}, u32[]{:S(2)}) copy-start(bf16[4,192,768]{2,1,0:T(8,128)(2,1)S(1)} %all-to-all-done) | copy-start | bytes 3538948
  24.9 82.0 %all-to-all-start.1 = ((bf16[32,32,384]{2,1,0:T(8,128)(2,1)}), bf16[32,32,384]{2,1,0:T(8,128)(2,1)S(1)}, u32[]{:S(2)}, u32[]{:S(2)}) async-start(bf16[32,32,384]{2,1,0:T(8,128)(2,1)} %broadcast_select_fusion), calls=%async_computation.1 | async-start | bytes 1572864 | tf_op jit(solution)/shard_map/all_to_all | solution.py:183
  43.0 132.3 %all-gather.8.cloned.1.call-start = ((), (), s32[]{:S(2)}) async-start(), calls=%async_computation.3 | async-start | bytes 3649536 | tf_op jit(solution)/shard_map/all_gather | solution.py:191
  106.9 2.1 copy-start.7
  109.8 93.1 %all-gather.10.cloned.1.call-start = ((), (), s32[]{:S(2)}) async-start(), calls=%async_computation.4 | async-start | bytes 3649536 | tf_op jit(solution)/shard_map/all_gather | solution.py:191
  111.7 8.9 %copy-start.3 = (bf16[528,384]{1,0:T(8,128)(2,1)S(1)}, bf16[528,384]{1,0:T(8,128)(2,1)}, u32[]{:S(2)}) copy-start(bf16[528,384]{1,0:T(8,128)(2,1)} %pad_maximum_fusion) | copy-start | bytes 1216516
  113.4 57.5 %copy-start.2 = (bf16[1344,768]{1,0:T(8,128)(2,1)}, bf16[1344,768]{1,0:T(8,128)(2,1)S(1)}, u32[]{:S(2)}) copy-start(bf16[1344,768]{1,0:T(8,128)(2,1)S(1)} %slice.23.refs_1_) | copy-start | bytes 6193156
  113.4 47.9 %collective-permute-start.1 = (bf16[1344,768]{1,0:T(8,128)(2,1)S(1)}, bf16[1344,768]{1,0:T(8,128)(2,1)}, u32[]{:S(2)}, u32[]{:S(2)}) collective-permute-start(bf16[1344,768]{1,0:T(8,128)(2,1)S(1)} %slice.23.refs_1_), channel_id=1, source_target_pairs={{0,16},{16,32},{32,48},{48,0},{1,17},{17,33},{33,49},{49,1},{2,18}... | collective-permute-start | bytes 6193160 | tf_op jit(solution)/shard_map/ppermute | solution.py:25
  116.8 45.9 %collective-permute-start.2 = (bf16[1344,768]{1,0:T(8,128)(2,1)S(1)}, bf16[1344,768]{1,0:T(8,128)(2,1)}, u32[]{:S(2)}, u32[]{:S(2)}) collective-permute-start(bf16[1344,768]{1,0:T(8,128)(2,1)S(1)} %slice.23.refs_1_), channel_id=1, source_target_pairs={{0,48},{16,0},{32,16},{48,32},{1,49},{17,1},{33,17},{49,33},{2,50}... | collective-permute-start | bytes 6193160 | tf_op jit(solution)/shard_map/ppermute | solution.py:25
  120.6 19.6 %collective-permute-start = (bf16[528,384]{1,0:T(8,128)(2,1)S(1)}, bf16[528,384]{1,0:T(8,128)(2,1)}, u32[]{:S(2)}, u32[]{:S(2)}) collective-permute-start(bf16[528,384]{1,0:T(8,128)(2,1)S(1)} %copy-done.3), channel_id=1, source_target_pairs={{0,8},{8,0},{1,9},{9,1},{2,10},{10,2},{3,11},{11,3},{4,12},{12,4},... | collective-permute-start | bytes 1216520 | tf_op jit(solution)/shard_map/ppermute | solution.py:25
  162.7 11.3 %copy-start.6 = (bf16[768]{0:T(1024)(128)(2,1)S(1)}, bf16[768]{0:T(1024)(128)(2,1)}, u32[]{:S(2)}) copy-start(bf16[768]{0:T(1024)(128)(2,1)} %param.11) | copy-start | bytes 4612
  165.1 27.8 %collective-permute-start.3 = (bf16[768,768]{1,0:T(8,128)(2,1)}, bf16[768,768]{1,0:T(8,128)(2,1)}, u32[]{:S(2)}, u32[]{:S(2)}) collective-permute-start(bf16[768,768]{1,0:T(8,128)(2,1)} %slice.24), channel_id=1, source_target_pairs={{0,16},{16,32},{32,48},{48,0},{1,17},{17,33},{33,49},{49,1},{2,18}... | collective-permute-start | bytes 3538952 | tf_op jit(solution)/shard_map/ppermute | solution.py:25
  170.9 19.7 %collective-permute-start.4 = (bf16[576,768]{1,0:T(8,128)(2,1)}, bf16[576,768]{1,0:T(8,128)(2,1)}, u32[]{:S(2)}, u32[]{:S(2)}) collective-permute-start(bf16[576,768]{1,0:T(8,128)(2,1)} %slice.25), channel_id=1, source_target_pairs={{0,48},{16,0},{32,16},{48,32},{1,49},{17,1},{33,17},{49,33},{2,50}... | collective-permute-start | bytes 2654216 | tf_op jit(solution)/shard_map/ppermute | solution.py:25
Sparse Core Ops, SparseCore 0:
  9.4 97.1 all-gather.5
  110.0 40.7 all-gather.7
  162.9 40.0 all-gather.9
